TPU v7x, 32 devices: a whole 2x2x4 slice. The times are simulated.
32 devices in a mesh: src: 2 (over core), brick: 16 (over z, y, x).
Axes of the slice: x: 2, y: 2, z: 4, core: 2. Of those that a mesh axis runs over, the one named last changes fastest.
Arguments:
- slowness: float32 [64, 64, 128], P('brick'), may hold values from 0.5 to 2
- source_x: int32 [4], P('src'), may hold values from 0 to 63
- source_y: int32 [4], P('src'), may hold values from 0 to 63
- source_z: int32 [4], P('src'), may hold values from 0 to 127
- station_x: int32 [2048], replicated, may hold values from 0 to 63
- station_y: int32 [2048], replicated, may hold values from 0 to 63
- station_z: int32 [2048], replicated, may hold values from 0 to 127
- observed: float32 [4, 2048], P('src'), may hold values from 0 to 4
Outputs:
- kernel: float32 [64, 64, 128], P('brick', 'src')
- arrivals: float32 [4, 2048], P('src', 'brick')
All inputs are finite; a program needn't handle non-finite values.
Results may differ from a plain program's by a relative error of at most 0.0003.
Values sent between devices are 32-bit elements; how exact they have to be, the bound alone decides.
A program may use at most 128 MiB of HBM per device.

v0:
```python
import functools

import jax
import jax.numpy as jnp
from jax import lax
from jax.experimental import pallas as pl
from jax.experimental.pallas import tpu as pltpu
from jax.sharding import PartitionSpec as P

ITERS = 16

spacing = 0.015625
big_value = 1000000.0
start_slowness = 2.0
half_step = 0.5 * spacing
LOW = 4
FORWARD = 8
GATHER_VMEM = 24 << 20
SOLVE_VMEM = 40 << 20
REDUCE_VMEM = 8 << 20
BACKWARD = 4

VMEM = pl.BlockSpec(memory_space=pltpu.VMEM)
SMEM = pl.BlockSpec(memory_space=pltpu.SMEM)
HBM = pl.BlockSpec(memory_space=pltpu.HBM)
MESH = pl.DeviceIdType.MESH


def remote(src, dst, send_sem, recv_sem, core, brick):
    return pltpu.make_async_remote_copy(
        src_ref=src,
        dst_ref=dst,
        send_sem=send_sem,
        recv_sem=recv_sem,
        device_id={"src": core, "brick": brick},
        device_id_type=MESH,
    )


def window(pair_depth, grid_x, margin):
    length = min(grid_x, pair_depth + 2 * margin)
    pair = lax.axis_index("brick") // 2
    return jnp.clip(pair * pair_depth - margin, 0, grid_x - length), length


def stations(grid_x, cells_y, pair_depth, stx_ref, sty_ref, stz_ref, obs_ref, cnt_ref, sum_ref, table):
    rec = stx_ref.shape[1]
    cells_z = cnt_ref.shape[2]
    rows_y = cells_y // 8
    shift = rows_y.bit_length() - 1
    low, length = window(pair_depth, grid_x, ITERS)
    parity = lax.rem(lax.axis_index("brick"), 2)
    sty = sty_ref[...]
    row = (stx_ref[...] - low) * cells_y + (sty & (rows_y - 1)) * 8 + (sty >> shift)
    seen = obs_ref[pl.ds(parity, 1), :]
    hi = seen.astype(jnp.bfloat16).astype(jnp.float32)
    rest = seen - hi
    mid = rest.astype(jnp.bfloat16).astype(jnp.float32)
    lo = rest - mid
    stz = stz_ref[...]
    hit = lax.broadcasted_iota(jnp.int32, (cells_z, rec), 0) == (stz & 1) * (cells_z // 2) + (stz >> 1)
    for part, value in enumerate((jnp.ones_like(seen), hi, mid, lo)):
        table[pl.ds(part * cells_z, cells_z), :] = jnp.where(hit, value, 0.0).astype(jnp.bfloat16)
    block = 256
    tiles = block // 8

    def tally(step):
        rows = lax.broadcasted_iota(jnp.int32, (block, rec), 0) + step * block
        pick = jnp.where(rows == row, 1.0, 0.0).astype(jnp.bfloat16)
        got = lax.dot_general(
            pick, table[...], (((1,), (1,)), ((), ())), preferred_element_type=jnp.float32
        )
        cnt_ref[pl.ds(step * tiles, tiles)] = got[:, :cells_z].reshape(tiles, 8, cells_z)
        total = got[:, cells_z : 2 * cells_z] + (
            got[:, 2 * cells_z : 3 * cells_z] + got[:, 3 * cells_z :]
        )
        sum_ref[pl.ds(step * tiles, tiles)] = total.reshape(tiles, 8, cells_z)

    return length * cells_y // block, tally


def gather_kernel(
    bricks,
    pair_depth,
    slow_ref,
    stx_ref,
    sty_ref,
    stz_ref,
    obs_ref,
    full_ref,
    cnt_ref,
    sum_ref,
    table,
    line_sem,
    send_sem,
    recv_sem,
    twin_sem,
    own_sem,
    stx_buf,
    sty_buf,
    stz_buf,
    obs_buf,
    in_sem,
):
    loads = [
        pltpu.make_async_copy(src, dst, in_sem.at[k])
        for k, (src, dst) in enumerate(
            ((stx_ref, stx_buf), (sty_ref, sty_buf), (stz_ref, stz_buf), (obs_ref, obs_buf))
        )
    ]
    for load in loads:
        load.start()
    depth = slow_ref.shape[0]
    half = depth // 2
    lines = bricks // LOW
    me = lax.axis_index("brick")
    core = lax.axis_index("src")
    h = lax.rem(core, 2)
    twin = core + 1 - 2 * h
    line = me // LOW
    bit_x = lax.rem(me, 2)
    bit_y = lax.rem(me // 2, 2)
    flip_x = 1 - 2 * bit_x
    flip_y = 2 - 4 * bit_y
    first = me + flip_x * (1 - h) + flip_y * h
    second = me + flip_y * (1 - h) + flip_x * h
    corner = me + flip_x + flip_y

    def piece(q, part):
        return full_ref.at[pl.ds(q * depth + part * half, half)]

    def copy(kind, q, brick, own=False):
        src = slow_ref.at[pl.ds(h * half, half)] if own else piece(q, h)
        return remote(src, piece(q, h), send_sem.at[kind, q], recv_sem.at[q], core, brick)

    def twin_copy(q):
        return remote(piece(q, h), piece(q, h), send_sem.at[2, q], twin_sem.at[q], twin, me)

    barrier = pltpu.get_barrier_semaphore()

    def greet(c, b):
        pl.semaphore_signal(barrier, inc=1, device_id={"src": c, "brick": b}, device_id_type=MESH)

    greet(twin, me)
    greet(core, first)
    greet(core, second)
    for k in range(1, lines):
        pl.when(line >= k)(lambda k=k: greet(core, me - LOW * k))
        pl.when(line + k < lines)(lambda k=k: greet(core, me + LOW * k))
    pl.semaphore_wait(barrier, lines + 2)

    def along(k, up):
        dst = piece(me, h)
        src = slow_ref.at[pl.ds(h * half, half)]
        brick = me + LOW * k if up else me - LOW * k
        return remote(src, dst, line_sem.at[int(up), k], recv_sem.at[me], core, brick)

    def own_line(k, wait):
        def go(up):
            c = along(k, up)
            c.wait_send() if wait else c.start()

        pl.when(line >= k)(lambda: go(False))
        pl.when(line + k < lines)(lambda: go(True))

    def sends(q, own, wait):
        for kind, brick in ((0, first), (1, second)):
            c = copy(kind, q, brick, own)
            c.wait_send() if wait else c.start()

    own_copy = pltpu.make_async_copy(slow_ref, full_ref.at[pl.ds(me * depth, depth)], own_sem)
    for k in range(1, lines):
        own_line(k, False)
        if k == 1:
            sends(me, True, False)
    own_copy.start()

    def arrived(q):
        remote(piece(q, h), piece(q, h), send_sem.at[0, q], recv_sem.at[q], core, first).wait_recv()

    def on_line(base, i, act):
        pl.when((i < lines) & (line >= i))(lambda: act(base - LOW * i, -1))
        pl.when((i < lines) & (line + i < lines))(lambda: act(base + LOW * i, 1))

    def both(base, i, act):
        pl.when(i == 0)(lambda: act(base, 0))
        pl.when(i > 0)(lambda: on_line(base, i, act))

    def from_line(wait):
        def act(q, side):
            if not wait:
                arrived(q)
            sends(q, False, wait)
            c = twin_copy(q)
            c.wait_send() if wait else c.start()

        return act

    def from_first(wait):
        def act(q, side):
            if not wait:
                arrived(q)
            c = copy(1, q, second)
            c.wait_send() if wait else c.start()
            c = twin_copy(q)
            c.wait_send() if wait else c.start()

        return act

    def from_second(wait):
        def act(q, side):
            if not wait:
                arrived(q)
            c = twin_copy(q)
            c.wait_send() if wait else c.start()

        return act

    def turn(i, wait):
        on_line(me, i, from_line(wait))
        both(first, i - 1, from_first(wait))
        both(second, i - 1, from_second(wait))
        pl.when(i >= 2)(lambda: both(corner, i - 2, from_second(wait)))

    grid_x, cells_y, _ = full_ref.shape
    for load in loads:
        load.wait()
    blocks, tally = stations(
        grid_x, cells_y, pair_depth, stx_buf, sty_buf, stz_buf, obs_buf, cnt_ref, sum_ref, table
    )
    early = 2
    rounds = lines + 1

    @pl.loop(0, early + rounds)
    def _(step):
        pl.when(step < blocks)(lambda: tally(step))
        pl.when(step >= early)(lambda: turn(step - early + 1, False))

    @pl.loop(early + rounds, max(blocks, early + rounds))
    def _(step):
        tally(step)

    own_copy.wait()
    sends(me, True, True)
    for k in range(1, lines):
        own_line(k, True)

    @pl.loop(1, lines + 2)
    def _(i):
        turn(i, True)

    @pl.loop(0, bricks)
    def _(q):
        @pl.when(q != me)
        def _():
            remote(piece(q, 1 - h), piece(q, 1 - h), send_sem.at[2, q], twin_sem.at[q], twin, me).wait_recv()


def solve_kernel(
    pair_depth,
    sx_ref,
    sy_ref,
    sz_ref,
    stx_hbm,
    sty_hbm,
    stz_hbm,
    slow_ref,
    cnt_ref,
    sum_ref,
    adj_ref,
    arr_ref,
    time,
    ping,
    pong,
    cost,
    picked,
    weight,
    supply,
    field,
    stx_ref,
    sty_ref,
    stz_ref,
    in_sem,
):
    loads = [
        pltpu.make_async_copy(src, dst, in_sem.at[k])
        for k, (src, dst) in enumerate(((stx_hbm, stx_ref), (sty_hbm, sty_ref), (stz_hbm, stz_ref)))
    ]
    for load in loads:
        load.start()
    grid_x, cells_y, cells_z = slow_ref.shape
    rows = cells_y // 8
    shift = rows.bit_length() - 1
    brick = lax.axis_index("brick")
    parity = lax.rem(brick, 2)
    pair = brick // 2
    lane = lax.broadcasted_iota(jnp.int32, (8, cells_z), 1)
    sub = lax.broadcasted_iota(jnp.int32, (8, cells_z), 0)
    lane_first = lane == 0
    lane_last = lane == cells_z - 1
    sub_first = sub == 0
    sub_last = sub == 7
    half_z = cells_z // 2
    upper = lane >= half_z
    index_up = jnp.where(lane_last, half_z - 1, jnp.where(upper, lane - half_z + 1, lane + half_z))
    index_down = jnp.where(lane_first, half_z, jnp.where(upper, lane - half_z, lane + half_z - 1))
    split = jnp.where(upper, (lane - half_z) * 2 + 1, lane * 2)
    join = (lane & 1) * half_z + (lane >> 1)

    def layer_of(ref, x):
        return tuple(ref[x * rows + v] for v in range(rows))

    def y_up(cur, v):
        return cur[v + 1] if v + 1 < rows else pltpu.roll(cur[0], 7, 0)

    def y_down(cur, v):
        return cur[v - 1] if v else pltpu.roll(cur[rows - 1], 1, 0)

    def z_up(one):
        return jnp.take_along_axis(one, index_up, axis=1)

    def z_down(one):
        return jnp.take_along_axis(one, index_down, axis=1)

    def swap(a, b):
        moved = pltpu.roll(jnp.where(upper, a, b), half_z, 1)
        return jnp.where(upper, moved, a), jnp.where(upper, b, moved)

    half_x = grid_x // 2
    sx = sx_ref[parity]
    sy = sy_ref[parity]
    sz = sz_ref[parity]
    shift_x = jnp.where(upper, half_x, 0) - sx
    z_even = jnp.where(upper, lane - half_z, lane) * 2 - sz
    flat = []
    for odd in range(2):
        dz = (z_even + odd).astype(jnp.float32)
        for v in range(rows):
            dy = (sub * rows + v - sy).astype(jnp.float32)
            flat.append(dy * dy + dz * dz)

    def slot(x, odd, v):
        return (x * 2 + odd) * rows + v

    @pl.loop(0, half_x)
    def _(x):
        dx = (x + shift_x).astype(jnp.float32)
        dx = dx * dx
        for v in range(rows):
            near = jnp.take_along_axis(slow_ref[x, pl.ds(v, 8, stride=rows), :], split, axis=1)
            far = jnp.take_along_axis(slow_ref[x + half_x, pl.ds(v, 8, stride=rows), :], split, axis=1)
            for odd, slow in enumerate(swap(near, far)):
                start = (start_slowness * spacing) * jnp.sqrt(dx + flat[odd * rows + v])
                cost[slot(x, odd, v)] = (2.0 * half_step) * slow
                ping[slot(x + 1, odd, v)] = start + half_step * slow

    inner = jnp.where(upper, lane - half_z, lane)
    far_index = (
        jnp.where(inner == 0, lane, lane - 1),
        jnp.where(inner == half_z - 1, lane, lane + 1),
    )

    def sweep(src, dst):
        for odd in range(2):
            for v in range(rows):
                first = pltpu.roll(src[slot(1, odd, v)], half_z, 1)
                last = pltpu.roll(src[slot(half_x, odd, v)], half_z, 1)
                src[slot(0, odd, v)] = jnp.where(upper, last, big_value)
                src[slot(half_x + 1, odd, v)] = jnp.where(upper, big_value, first)

        @pl.loop(0, half_x // FORWARD)
        def _(i):
            for j in range(FORWARD):
                x = i * FORWARD + j
                cur = [[src[slot(x + 1, odd, v)] for v in range(rows)] for odd in range(2)]
                for v in range(rows):
                    for odd in range(2):
                        one = cur[odd][v]
                        pair_z = cur[1 - odd][v]
                        up = y_up(cur[odd], v)
                        down = y_down(cur[odd], v)
                        if v + 1 == rows:
                            up = jnp.where(sub_last, big_value, up)
                        if v == 0:
                            down = jnp.where(sub_first, big_value, down)
                        far_z = jnp.take_along_axis(pair_z, far_index[odd], axis=1)
                        along_x = jnp.minimum(src[slot(x, odd, v)], src[slot(x + 2, odd, v)])
                        low = jnp.minimum(
                            jnp.minimum(along_x, jnp.minimum(up, down)), jnp.minimum(pair_z, far_z)
                        )
                        dst[slot(x + 1, odd, v)] = jnp.minimum(one, low + cost[slot(x, odd, v)])

    assert ITERS % 2 == 0

    @pl.loop(0, ITERS // 2)
    def _(_step):
        sweep(ping, pong)
        sweep(pong, ping)

    @pl.loop(0, half_x)
    def _(x):
        for v in range(rows):
            even, odd = (ping[slot(x + 1, k, v)] - 0.5 * cost[slot(x, k, v)] for k in range(2))
            near, far = swap(even, odd)
            time[(x + 1) * rows + v] = near
            time[(x + half_x + 1) * rows + v] = far

    for v in range(rows):
        time[v] = jnp.full((8, cells_z), -big_value, jnp.float32)
        time[(grid_x + 1) * rows + v] = jnp.full((8, cells_z), -big_value, jnp.float32)

    for load in loads:
        load.wait()

    count = picked.shape[0]
    line = lax.broadcasted_iota(jnp.int32, (1, cells_z), 1)
    unroll = 8

    @pl.loop(0, count // unroll)
    def _(i):
        for j in range(unroll):
            r = pair * count + i * unroll + j
            y = sty_ref[r]
            z = stz_ref[r]
            at = (stx_ref[r] + 1) * rows + (y & (rows - 1))
            got = time[at, pl.ds(y >> shift, 1), :]
            picked[pl.ds(i * unroll + j, 1), :] = jnp.where(line == (z & 1) * half_z + (z >> 1), got, 0.0)

    arrived = jnp.sum(jnp.transpose(picked[...]), axis=0, keepdims=True)
    arr_ref[0] = arrived[:, : count // 2]
    arr_ref[1] = arrived[:, count // 2 :]

    base, length = window(pair_depth, grid_x, ITERS - 1)
    outer, _ = window(pair_depth, grid_x, ITERS)

    def weigh(x, prev, cur):
        nxt = layer_of(time, x + 2)
        spot = (x - base) * rows
        for v in range(rows):
            one = cur[v]

            def gain(other):
                return jnp.maximum(other - one, 0.0)

            up = gain(y_up(cur, v))
            down = gain(y_down(cur, v))
            if v + 1 == rows:
                up = jnp.where(sub_last, 0.0, up)
            if v == 0:
                down = jnp.where(sub_first, 0.0, down)
            parts = (
                gain(prev[v]),
                gain(nxt[v]),
                down,
                up,
                jnp.where(lane_first, 0.0, gain(z_down(one))),
                jnp.where(lane_last, 0.0, gain(z_up(one))),
            )
            total = ((parts[0] + parts[1]) + (parts[2] + parts[3])) + (parts[4] + parts[5])
            inverse = 1.0 / (1.0 + total * (1.0 / spacing))
            scaled = inverse * (1.0 / spacing)
            for k, part in enumerate(parts):
                weight[k, spot + v] = part * scaled
            here = (x - outer) * rows + v
            value = (cnt_ref[here] * one - sum_ref[here]) * inverse
            supply[spot + v] = value
            field[spot + rows + v] = value
        return nxt

    def weigh_body(i, carry):
        prev, cur = carry
        for j in range(2):
            nxt = weigh(base + i * 2 + j, prev, cur)
            prev, cur = cur, nxt
        return prev, cur

    lax.fori_loop(0, length // 2, weigh_body, (layer_of(time, base), layer_of(time, base + 1)))
    for v in range(rows):
        field[v] = jnp.zeros((8, cells_z), jnp.float32)
        field[(length + 1) * rows + v] = jnp.zeros((8, cells_z), jnp.float32)

    def backward(x, prev, cur):
        nxt = layer_of(field, x + 2)
        for v in range(rows):
            one = cur[v]
            spot = x * rows + v
            acc = supply[spot] + weight[0, spot] * prev[v]
            acc = acc + weight[1, spot] * nxt[v]
            side = weight[2, spot] * y_down(cur, v) + weight[3, spot] * y_up(cur, v)
            acc = acc + side
            acc = acc + (weight[4, spot] * z_down(one) + weight[5, spot] * z_up(one))
            field[spot + rows] = acc
        return nxt

    @pl.loop(2, ITERS + 1)
    def _(sweep):
        margin = ITERS - sweep
        span = jnp.minimum(grid_x, (pair_depth + 2 * margin + BACKWARD - 1) // BACKWARD * BACKWARD)
        first = jnp.clip(pair * pair_depth - margin, 0, grid_x - span) - base

        def body(i, carry):
            prev, cur = carry
            for j in range(BACKWARD):
                nxt = backward(first + i * BACKWARD + j, prev, cur)
                prev, cur = cur, nxt
            return prev, cur

        lax.fori_loop(0, span // BACKWARD, body, (layer_of(field, first), layer_of(field, first + 1)))

    mine = pair * pair_depth - base + 1
    for x in range(pair_depth):
        for v in range(rows):
            adj_ref[x, pl.ds(v, 8, stride=rows), :] = jnp.take_along_axis(
                field[(mine + x) * rows + v], join, axis=1
            )


def reduce_kernel(cores, adj_ref, arr_ref, out_ref, got_ref, slots, send_sem, recv_sem, word_send, word_recv):
    depth, keep, _ = out_ref.shape
    brick = lax.axis_index("brick")
    core = lax.axis_index("src")
    parity = lax.rem(brick, 2)
    other = brick + 1 - 2 * parity
    me = core * 2 + parity

    def target(k):
        c = lax.rem(core + k // 2, cores)
        p = lax.rem(parity + k % 2, 2)
        return c, p, brick - parity + p

    def copy(k):
        c, p, b = target(k)
        return remote(
            adj_ref.at[pl.ds(p * depth, depth), pl.ds(c * keep, keep)],
            slots.at[k],
            send_sem.at[k],
            recv_sem.at[k],
            c,
            b,
        )

    barrier = pltpu.get_barrier_semaphore()
    for k in range(1, 2 * cores):
        c, _, b = target(k)
        pl.semaphore_signal(barrier, inc=1, device_id={"src": c, "brick": b}, device_id_type=MESH)
    pl.semaphore_wait(barrier, 2 * cores - 1)
    word = remote(arr_ref.at[1 - parity], got_ref.at[parity], word_send, word_recv, core, other)
    word.start()
    for k in range(1, 2 * cores):
        copy(k).start()
    got_ref[parity] = arr_ref[parity]
    total = adj_ref[pl.ds(parity * depth, depth), pl.ds(pl.multiple_of(core * keep, 8), keep), :]
    for k in range(1, 2 * cores):
        copy(k).wait_recv()
        total = total + slots[k]
    out_ref[...] = total
    for k in range(1, 2 * cores):
        copy(k).wait_send()
    word.wait_send()
    remote(arr_ref.at[parity], got_ref.at[1 - parity], word_send, word_recv, core, other).wait_recv()


def per_device(slowness, source_x, source_y, source_z, station_x, station_y, station_z, observed):
    bricks = lax.axis_size("brick")
    cores = lax.axis_size("src")
    depth, cells_y, cells_z = slowness.shape
    grid_x = depth * bricks
    rec = station_x.shape[0]
    pair_depth = 2 * depth
    rows = cells_y // 8
    assert source_x.shape[0] == 2 and bricks % LOW == 0 and cores % 2 == 0
    f32 = jnp.float32

    wide = min(grid_x, pair_depth + 2 * ITERS)
    field = jax.ShapeDtypeStruct((wide * rows, 8, cells_z), f32)
    full, cnt, total = pl.pallas_call(
        functools.partial(gather_kernel, bricks, pair_depth),
        name="gather",
        out_shape=(jax.ShapeDtypeStruct((grid_x, cells_y, cells_z), f32), field, field),
        in_specs=[VMEM] + [HBM] * 4,
        out_specs=(VMEM, VMEM, VMEM),
        scratch_shapes=[
            pltpu.VMEM((4 * cells_z, rec), jnp.bfloat16),
            pltpu.SemaphoreType.DMA((2, bricks // LOW)),
            pltpu.SemaphoreType.DMA((3, bricks)),
            pltpu.SemaphoreType.DMA((bricks,)),
            pltpu.SemaphoreType.DMA((bricks,)),
            pltpu.SemaphoreType.DMA,
            pltpu.VMEM((1, rec), jnp.int32),
            pltpu.VMEM((1, rec), jnp.int32),
            pltpu.VMEM((1, rec), jnp.int32),
            pltpu.VMEM(observed.shape, f32),
            pltpu.SemaphoreType.DMA((4,)),
        ],
        compiler_params=pltpu.CompilerParams(
            collective_id=0, has_side_effects=True, vmem_limit_bytes=GATHER_VMEM
        ),
    )(slowness, station_x[None], station_y[None], station_z[None], observed)

    length = min(grid_x, pair_depth + 2 * (ITERS - 1))
    share = rec // bricks
    adj, arr = pl.pallas_call(
        functools.partial(solve_kernel, pair_depth),
        name="solve",
        out_shape=(
            jax.ShapeDtypeStruct((pair_depth, cells_y, cells_z), f32),
            jax.ShapeDtypeStruct((2, 1, share), f32),
        ),
        in_specs=[SMEM] * 3 + [HBM] * 3 + [VMEM] * 3,
        out_specs=(VMEM, VMEM),
        scratch_shapes=[
            pltpu.VMEM(((grid_x + 2) * rows, 8, cells_z), f32),
            pltpu.VMEM(((grid_x + 4) * rows, 8, cells_z), f32),
            pltpu.VMEM(((grid_x + 4) * rows, 8, cells_z), f32),
            pltpu.VMEM((grid_x * rows, 8, cells_z), f32),
            pltpu.VMEM((2 * share, cells_z), f32),
            pltpu.VMEM((6, length * rows, 8, cells_z), f32),
            pltpu.VMEM((length * rows, 8, cells_z), f32),
            pltpu.VMEM(((length + 2) * rows, 8, cells_z), f32),
            pltpu.SMEM((rec,), jnp.int32),
            pltpu.SMEM((rec,), jnp.int32),
            pltpu.SMEM((rec,), jnp.int32),
            pltpu.SemaphoreType.DMA((3,)),
        ],
        compiler_params=pltpu.CompilerParams(vmem_limit_bytes=SOLVE_VMEM),
    )(source_x, source_y, source_z, station_x, station_y, station_z, full, cnt, total)

    keep = cells_y // cores
    summed, arrivals = pl.pallas_call(
        functools.partial(reduce_kernel, cores),
        name="reduce",
        out_shape=(
            jax.ShapeDtypeStruct((depth, keep, cells_z), f32),
            jax.ShapeDtypeStruct((2, 1, share), f32),
        ),
        in_specs=[VMEM, VMEM],
        out_specs=(VMEM, VMEM),
        scratch_shapes=[
            pltpu.VMEM((2 * cores, depth, keep, cells_z), f32),
            pltpu.SemaphoreType.DMA((2 * cores,)),
            pltpu.SemaphoreType.DMA((2 * cores,)),
            pltpu.SemaphoreType.DMA,
            pltpu.SemaphoreType.DMA,
        ],
        compiler_params=pltpu.CompilerParams(
            collective_id=1, has_side_effects=True, vmem_limit_bytes=REDUCE_VMEM
        ),
    )(adj, arr)
    own = lax.dynamic_slice_in_dim(slowness, lax.axis_index("src") * keep, keep, axis=1)
    return own * summed, arrivals[:, 0]


def solution(mesh):
    in_specs = (P("brick", None, None), P("src"), P("src"), P("src"), P(), P(), P(), P("src", None))
    out_specs = (P("brick", "src", None), P("src", "brick"))
    return jax.shard_map(
        per_device, mesh=mesh, in_specs=in_specs, out_specs=out_specs, check_vma=False
    )
```

profile of v0, /device:TPU:0, one launch (start us, length us, event | category | flops | bytes accessed | tf_op | source)
XLA Modules:
  0.0 79.8 jit_solution(13356869540199301322)
XLA Ops:
  0.6 0.0 copy-start
  0.6 0.9 %copy-done = f32[4,64,128]{2,1,0:T(8,128)S(1)} copy-done((f32[4,64,128]{2,1,0:T(8,128)S(1)}, f32[4,64,128]{2,1,0:T(8,128)}, u32[]{:S(2)}) %copy-start) | copy-done | bytes 131096
  1.5 0.0 copy-start.2
  1.5 0.7 copy-done.2
  2.2 0.0 copy-start.4
  2.2 0.7 copy-done.4
  2.9 0.0 copy-start.6
  2.9 0.7 copy-done.6
  3.6 0.0 copy-start.8
  3.6 0.7 copy-done.8
  4.3 24.5 %gather.1 = (f32[64,64,128]{2,1,0:T(8,128)S(1)}, f32[320,8,128]{2,1,0:T(8,128)S(1)}, f32[320,8,128]{2,1,0:T(8,128)S(1)}) custom-call(f32[4,64,128]{2,1,0:T(8,128)S(1)} %copy-done, s32[1,2048]{1,0:T(1,128)S(1)} %bitcast.4, s32[1,2048]{1,0:T(1,128)S(1)} %bitcast.5, s32[1,2048]{1,0:T(1,128)S(1)} %bitcast.6, f32[2,2048]{1,0:T(2,128)S(1)} %copy-done.8), custom_call_target="tpu_custom_call" | custom-call | tf_op jit(solution)/shard_map/gather/pallas_call | solution.py:576
  28.9 0.0 copy-start.3
  28.9 0.7 copy-done.3
  29.6 0.0 copy-start.5
  29.6 0.7 copy-done.5
  30.3 0.0 copy-start.7
  30.3 0.7 copy-done.7
  31.0 0.0 copy-start.9
  31.0 0.7 copy-done.9
  31.6 0.0 copy-start.10
  31.6 0.7 copy-done.10
  32.3 0.0 copy-start.11
  32.3 0.7 copy-done.11
  33.0 0.0 copy-start.1
  33.0 40.2 %solve.1 = (f32[8,64,128]{2,1,0:T(8,128)S(1)}, f32[2,1,128]{2,1,0:T(1,128)S(1)}) custom-call(s32[2]{0:T(128)S(1)} %copy-done.9, s32[2]{0:T(128)S(1)} %copy-done.10, s32[2]{0:T(128)S(1)} %copy-done.11, s32[2048]{0:T(1024)S(1)} %copy-done.3, s32[2048]{0:T(1024)S(1)} %copy-done.5, s32[2048]{0:T(1024)S(1)} %copy-done.7, ...), custom_call_target="tpu_custom_call" | custom-call | tf_op jit(solution)/shard_map/solve/pallas_call | solution.py:602
  73.2 5.4 %reduce.1 = (f32[4,32,128]{2,1,0:T(8,128)S(1)}, f32[2,1,128]{2,1,0:T(1,128)S(1)}) custom-call(f32[8,64,128]{2,1,0:T(8,128)S(1)} %get-tuple-element.12.adj_ref, f32[2,1,128]{2,1,0:T(1,128)S(1)} %get-tuple-element.13.arr_ref), custom_call_target="tpu_custom_call" | custom-call | tf_op jit(solution)/shard_map/reduce/pallas_call | solution.py:629
  78.6 0.0 copy-done.1
  78.6 0.6 dynamic-slice_multiply_fusion
  79.2 0.6 copy.11
Async XLA Ops:
  0.6 0.9 %copy-start = (f32[4,64,128]{2,1,0:T(8,128)S(1)}, f32[4,64,128]{2,1,0:T(8,128)}, u32[]{:S(2)}) copy-start(f32[4,64,128]{2,1,0:T(8,128)} %slow_ref.1) | copy-start | bytes 393220
  1.5 0.7 copy-start.2
  2.2 0.7 copy-start.4
  2.9 0.7 copy-start.6
  3.6 0.7 copy-start.8
  28.9 0.7 copy-start.3
  29.6 0.7 copy-start.5
  30.3 0.7 copy-start.7
  31.0 0.7 copy-start.9
  31.6 0.7 copy-start.10
  32.3 0.7 copy-start.11
  33.0 45.6 %copy-start.1 = (f32[4,64,128]{2,1,0:T(8,128)S(1)}, f32[4,64,128]{2,1,0:T(8,128)}, u32[]{:S(2)}) copy-start(f32[4,64,128]{2,1,0:T(8,128)} %slow_ref.1) | copy-start | bytes 393220
where the time goes:
time: 80.4 us; the launch traced here: 79.8 us
  Pallas kernels  70.1 us (87%)
  local copies, waits for them, and re-layouts  8.32 us (10%)
    pallas_call x1, Pallas kernels, per_device(): pl.pallas_call(functools.partial(solve_kernel, pair_depth), name='solve',...  40.2 us
    pallas_call x1, Pallas kernels, per_device(): pl.pallas_call(functools.partial(gather_kernel, bricks, pair_depth), name...  24.5 us
    unnamed x25, local copies, waits for them, and re-layouts  8.32 us
    pallas_call x1, Pallas kernels, per_device(): pl.pallas_call(functools.partial(reduce_kernel, cores), name='reduce', ou...  5.41 us

commit v1 on v0

v1 whole, which is shorter than its diff:
```python
import functools

import jax
import jax.numpy as jnp
from jax import lax
from jax.experimental import pallas as pl
from jax.experimental.pallas import tpu as pltpu
from jax.sharding import PartitionSpec as P

ITERS = 16

spacing = 0.015625
big_value = 1000000.0
start_slowness = 2.0
half_step = 0.5 * spacing
LOW = 4
GATHER_VMEM = 24 << 20
SOLVE_VMEM = 44 << 20
FINISH_VMEM = 8 << 20
TALLY = 512

VMEM = pl.BlockSpec(memory_space=pltpu.VMEM)
SMEM = pl.BlockSpec(memory_space=pltpu.SMEM)
HBM = pl.BlockSpec(memory_space=pltpu.HBM)
MESH = pl.DeviceIdType.MESH


def remote(src, dst, send_sem, recv_sem, core, brick):
    return pltpu.make_async_remote_copy(
        src_ref=src,
        dst_ref=dst,
        send_sem=send_sem,
        recv_sem=recv_sem,
        device_id={"src": core, "brick": brick},
        device_id_type=MESH,
    )


def gather_kernel(
    bricks,
    slow_ref,
    sx_ref,
    sy_ref,
    sz_ref,
    stx_ref,
    sty_ref,
    stz_ref,
    obs_ref,
    full_ref,
    tally_ref,
    code_ref,
    spot_ref,
    table,
    line_sem,
    send_sem,
    recv_sem,
    twin_sem,
    own_sem,
    stx_buf,
    sty_buf,
    stz_buf,
    seen_buf,
    sx_buf,
    sy_buf,
    sz_buf,
    in_sem,
    word_send,
    word_recv,
):
    depth = slow_ref.shape[0]
    half = depth // 2
    lines = bricks // LOW
    me = lax.axis_index("brick")
    core = lax.axis_index("src")
    h = lax.rem(core, 2)
    twin = core + 1 - 2 * h
    line = me // LOW
    place = lax.rem(me, LOW)
    bit_x = lax.rem(me, 2)
    bit_y = lax.rem(me // 2, 2)
    flip_x = 1 - 2 * bit_x
    flip_y = 2 - 4 * bit_y
    first = me + flip_x * (1 - h) + flip_y * h
    second = me + flip_y * (1 - h) + flip_x * h
    corner = me + flip_x + flip_y
    owner = place // 2 == h
    local = lax.rem(place, 2)

    barrier = pltpu.get_barrier_semaphore()

    def greet(c, b):
        pl.semaphore_signal(barrier, inc=1, device_id={"src": c, "brick": b}, device_id_type=MESH)

    greet(twin, me)
    greet(core, first)
    greet(core, second)
    for k in range(1, lines):
        pl.when(line >= k)(lambda k=k: greet(core, me - LOW * k))
        pl.when(line + k < lines)(lambda k=k: greet(core, me + LOW * k))

    stations = [
        pltpu.make_async_copy(src, dst, in_sem.at[k])
        for k, (src, dst) in enumerate(((stx_ref, stx_buf), (sty_ref, sty_buf), (stz_ref, stz_buf)))
    ]
    spots = [
        pltpu.make_async_copy(src, dst, in_sem.at[3 + k])
        for k, (src, dst) in enumerate(((sx_ref, sx_buf), (sy_ref, sy_buf), (sz_ref, sz_buf)))
    ]
    seen_copy = pltpu.make_async_copy(obs_ref, seen_buf, in_sem.at[6])
    for load in stations:
        load.start()

    @pl.when(owner)
    def _():
        for load in spots:
            load.start()
        seen_copy.start()

    def piece(q, part):
        return full_ref.at[pl.ds(q * depth + part * half, half)]

    def copy(kind, q, brick, own=False):
        src = slow_ref.at[pl.ds(h * half, half)] if own else piece(q, h)
        return remote(src, piece(q, h), send_sem.at[kind, q], recv_sem.at[q], core, brick)

    def twin_copy(q):
        return remote(piece(q, h), piece(q, h), send_sem.at[2, q], twin_sem.at[q], twin, me)

    def along(k, up):
        dst = piece(me, h)
        src = slow_ref.at[pl.ds(h * half, half)]
        brick = me + LOW * k if up else me - LOW * k
        return remote(src, dst, line_sem.at[int(up), k], recv_sem.at[me], core, brick)

    def own_line(k, wait):
        def go(up):
            c = along(k, up)
            c.wait_send() if wait else c.start()

        pl.when(line >= k)(lambda: go(False))
        pl.when(line + k < lines)(lambda: go(True))

    def sends(q, own, wait):
        for kind, brick in ((0, first), (1, second)):
            c = copy(kind, q, brick, own)
            c.wait_send() if wait else c.start()

    own_copy = pltpu.make_async_copy(slow_ref, full_ref.at[pl.ds(me * depth, depth)], own_sem)
    seen_send = remote(obs_ref, seen_buf, word_send.at[0], word_recv.at[0], twin, me)
    spot_send = remote(spot_ref, spot_ref, word_send.at[1], word_recv.at[1], twin, me)

    pl.semaphore_wait(barrier, lines + 2)
    pl.when(owner)(seen_send.start)
    for k in range(1, lines):
        own_line(k, False)
        if k == 1:
            sends(me, True, False)
    own_copy.start()

    def arrived(q):
        remote(piece(q, h), piece(q, h), send_sem.at[0, q], recv_sem.at[q], core, first).wait_recv()

    def on_line(base, i, act):
        pl.when((i < lines) & (line >= i))(lambda: act(base - LOW * i, -1))
        pl.when((i < lines) & (line + i < lines))(lambda: act(base + LOW * i, 1))

    def both(base, i, act):
        pl.when(i == 0)(lambda: act(base, 0))
        pl.when(i > 0)(lambda: on_line(base, i, act))

    def from_line(wait):
        def act(q, side):
            if not wait:
                arrived(q)
            sends(q, False, wait)
            c = twin_copy(q)
            c.wait_send() if wait else c.start()

        return act

    def from_first(wait):
        def act(q, side):
            if not wait:
                arrived(q)
            c = copy(1, q, second)
            c.wait_send() if wait else c.start()
            c = twin_copy(q)
            c.wait_send() if wait else c.start()

        return act

    def from_second(wait):
        def act(q, side):
            if not wait:
                arrived(q)
            c = twin_copy(q)
            c.wait_send() if wait else c.start()

        return act

    def turn(i, wait):
        on_line(me, i, from_line(wait))
        both(first, i - 1, from_first(wait))
        both(second, i - 1, from_second(wait))
        pl.when(i >= 2)(lambda: both(corner, i - 2, from_second(wait)))

    @pl.when(owner)
    def _():
        for load in spots:
            load.wait()
        sub = lax.broadcasted_iota(jnp.int32, spot_ref.shape, 0)
        spot_ref[...] = jnp.where(
            sub == 0, sx_buf[local], jnp.where(sub == 1, sy_buf[local], sz_buf[local])
        )

    for load in stations:
        load.wait()
    grid_x, cells_y, cells_z = full_ref.shape
    rows = cells_y // 8
    shift = rows.bit_length() - 1
    ring = grid_x // 2
    centre = line * (LOW * depth) + LOW * depth // 2
    sty = sty_buf[...]
    stz = stz_buf[...]
    stx = stx_buf[...]
    away = stx - centre
    away = jnp.where(away < 0, away + grid_x, away)
    upper = away < ring
    step_x = jnp.where(upper, away, grid_x - 1 - away)
    row = (step_x * rows + (sty & (rows - 1))) * 8 + (sty >> shift)
    column = jnp.where(upper, cells_z // 2, 0) + (stz >> 1)
    column = jnp.where(((stx + sty + stz) & 1) == h, column, -1)
    code_ref[0] = row
    code_ref[1] = column
    rec = row.shape[1]
    hit = lax.broadcasted_iota(jnp.int32, (cells_z, rec), 0) == column

    pl.when(owner)(seen_copy.wait)
    pl.when(owner)(spot_send.start)
    pl.when(jnp.logical_not(owner))(seen_send.wait_recv)
    seen = seen_buf[pl.ds(local, 1), :] * (1.0 / spacing)
    hi = seen.astype(jnp.bfloat16).astype(jnp.float32)
    rest = seen - hi
    mid = rest.astype(jnp.bfloat16).astype(jnp.float32)
    lo = rest - mid
    for part, value in enumerate((jnp.ones_like(seen), hi, mid, lo)):
        table[pl.ds(part * cells_z, cells_z), :] = jnp.where(hit, value, 0.0).astype(jnp.bfloat16)

    tiles = TALLY // 8
    blocks = tally_ref.shape[1] // tiles

    def tally(step):
        rows_of = lax.broadcasted_iota(jnp.int32, (TALLY, rec), 0) + step * TALLY
        pick = jnp.where(rows_of == row, 1.0, 0.0).astype(jnp.bfloat16)
        got = lax.dot_general(
            pick, table[...], (((1,), (1,)), ((), ())), preferred_element_type=jnp.float32
        )
        spot = pl.ds(step * tiles, tiles)
        tally_ref[0, spot] = got[:, :cells_z].reshape(tiles, 8, cells_z)
        total = got[:, cells_z : 2 * cells_z] + (
            got[:, 2 * cells_z : 3 * cells_z] + got[:, 3 * cells_z :]
        )
        tally_ref[1, spot] = total.reshape(tiles, 8, cells_z)

    rounds = lines + 1
    tally_send = remote(
        tally_ref.at[pl.ds(0, 2)], tally_ref.at[pl.ds(2, 2)], word_send.at[2], word_recv.at[2], twin, me
    )

    @pl.loop(0, max(rounds, blocks + 1))
    def _(step):
        pl.when(step < blocks)(lambda: tally(step))
        pl.when(step < rounds)(lambda: turn(step + 1, False))
        pl.when(step == blocks)(tally_send.start)

    own_copy.wait()
    sends(me, True, True)
    for k in range(1, lines):
        own_line(k, True)

    @pl.loop(1, lines + 2)
    def _(i):
        turn(i, True)

    @pl.loop(0, bricks)
    def _(q):
        @pl.when(q != me)
        def _():
            remote(piece(q, 1 - h), piece(q, 1 - h), send_sem.at[2, q], twin_sem.at[q], twin, me).wait_recv()

    tally_send.wait()

    @pl.when(owner)
    def _():
        seen_send.wait_send()
        spot_send.wait_send()

    pl.when(jnp.logical_not(owner))(spot_send.wait_recv)


def solve_kernel(
    depth,
    cores,
    code_ref,
    spot_ref,
    full_ref,
    tally_ref,
    slots_ref,
    got_ref,
    chain,
    other,
    chain_cost,
    other_cost,
    twin_time,
    chain_weight,
    other_weight,
    chain_supply,
    other_supply,
    chain_field,
    other_field,
    packed,
    picked,
    part,
    code,
    code_sem,
    time_send,
    time_recv,
    send_sem,
    recv_sem,
    part_send,
    part_recv,
    self_sem,
):
    grid_x, cells_y, cells_z = full_ref.shape
    rows = cells_y // 8
    ring = grid_x // 2
    block = LOW * depth
    half = block // 2
    span = half + ITERS
    brick = lax.axis_index("brick")
    core = lax.axis_index("src")
    h = lax.rem(core, 2)
    twin = core + 1 - 2 * h
    group = brick // LOW
    place = lax.rem(brick, LOW)
    base = group * LOW
    peers = LOW * cores
    mine = core * LOW + place
    centre = group * block + half
    half_z = cells_z // 2

    barrier = pltpu.get_barrier_semaphore()

    def peer(k):
        t = lax.rem(mine + k, peers)
        return t // LOW, base + lax.rem(t, LOW), lax.rem(t, LOW)

    for k in range(1, peers):
        c, b, _ = peer(k)
        pl.semaphore_signal(barrier, inc=1, device_id={"src": c, "brick": b}, device_id_type=MESH)

    share = got_ref.shape[-1]
    quarter = picked.shape[0]
    load_code = pltpu.make_async_copy(code_ref.at[0], code, code_sem)
    load_code.start()

    lane = lax.broadcasted_iota(jnp.int32, (8, cells_z), 1)
    sub = lax.broadcasted_iota(jnp.int32, (8, cells_z), 0)
    sub_first = sub == 0
    sub_last = sub == 7
    upper = lane >= half_z
    inner = jnp.where(upper, lane - half_z, lane)
    parity = [lax.rem(q + h, 2) for q in range(2)]
    cell_z = [inner * 2 + jnp.where(upper, 1 - p, p) for p in parity]
    from_low = [(lane & 1) == p for p in parity]
    slide = [inner + jnp.where(upper, 1, -1) * (1 - 2 * p) for p in parity]
    edge_z = [(s < 0) | (s >= half_z) for s in slide]
    far = [jnp.where(upper, half_z, 0) + jnp.clip(s, 0, half_z - 1) for s in slide]

    def slot(i, v):
        return (i + 1) * rows + v

    sx = spot_ref[0:1, :]
    sy = spot_ref[1:2, :]
    sz = spot_ref[2:3, :]
    unit = (start_slowness * spacing) ** 2
    flat = []
    for q in range(2):
        dz = (cell_z[q] - sz).astype(jnp.float32)
        dz = dz * dz
        for v in range(rows):
            dy = (sub * rows + v - sy).astype(jnp.float32)
            flat.append((dy * dy + dz) * unit)

    @pl.loop(0, ring // 2)
    def _(pair):
        for j in range(2):
            i = pair * 2 + j
            x_low = centre - 1 - i
            x_low = jnp.where(x_low < 0, x_low + grid_x, x_low)
            x_high = centre + i
            x_high = jnp.where(x_high >= grid_x, x_high - grid_x, x_high)
            dx = (jnp.where(upper, x_high, x_low) - sx).astype(jnp.float32)
            dx = dx * dx * unit
            for v in range(rows):
                q = (j + 1 + v) % 2
                low = full_ref[x_low, pl.ds(v, 8, stride=rows), :]
                high = full_ref[x_high, pl.ds(v, 8, stride=rows), :]
                for field, cost, k, natural in (
                    (chain, chain_cost, q, jnp.where(from_low[q], low, high)),
                    (other, other_cost, 1 - q, jnp.where(from_low[q], high, low)),
                ):
                    slow = jnp.take_along_axis(natural, cell_z[k], axis=1)
                    square = dx + flat[k * rows + v]
                    start = square * lax.rsqrt(jnp.maximum(square, unit * 0.5))
                    cost[i * rows + v] = (2.0 * half_step) * slow
                    field[slot(i, v)] = start + half_step * slow

    cuts = {
        b: jnp.where(upper, grid_x - centre, centre) == b for b in range(half, ring, half) if (b // half) % 2
    }

    def swing(one):
        return pltpu.roll(one, half_z, 1)

    def y_up(cur, v):
        return cur[v + 1] if v + 1 < rows else pltpu.roll(cur[0], 7, 0)

    def y_down(cur, v):
        return cur[v - 1] if v else pltpu.roll(cur[rows - 1], 1, 0)

    def sweep(dst, cost, src, turned):
        for i in range(ring):
            cur = [src[slot(i, v)] for v in range(rows)]
            for v in range(rows):
                q = (i + 1 + v) % 2
                before = src[slot(i - 1, v)] if i else swing(cur[v])
                after = src[slot(i + 1, v)] if i + 1 < ring else swing(cur[v])
                if i in cuts:
                    before = jnp.where(cuts[i], big_value, before)
                if i + 1 in cuts:
                    after = jnp.where(cuts[i + 1], big_value, after)
                up = y_up(cur, v)
                down = y_down(cur, v)
                if v + 1 == rows:
                    up = jnp.where(sub_last, big_value, up)
                if v == 0:
                    down = jnp.where(sub_first, big_value, down)
                across = jnp.take_along_axis(cur[v], far[q ^ turned], axis=1)
                low = jnp.minimum(
                    jnp.minimum(jnp.minimum(before, after), jnp.minimum(up, down)),
                    jnp.minimum(cur[v], across),
                )
                dst[slot(i, v)] = jnp.minimum(dst[slot(i, v)], low + cost[i * rows + v])

    assert ITERS % 2 == 0

    @pl.loop(0, ITERS // 2)
    def _(_step):
        sweep(other, other_cost, chain, 1)
        sweep(chain, chain_cost, other, 0)

    @pl.loop(0, ring)
    def _(i):
        for v in range(rows):
            chain[slot(i, v)] = (chain[slot(i, v)] - 0.5 * chain_cost[i * rows + v]) * (1.0 / spacing)

    for v in range(rows):
        chain[slot(-1, v)] = swing(chain[slot(0, v)])

    pl.semaphore_wait(barrier, peers - 1)
    reach = span + 2
    time_copy = remote(
        chain.at[pl.ds(0, reach * rows)], twin_time, time_send, time_recv, twin, brick
    )
    time_copy.start()

    load_code.wait()
    unroll = 16

    @pl.loop(0, quarter // unroll)
    def _(n):
        for j in range(unroll):
            r = n * unroll + j
            at = code[0, group * quarter + r]
            picked[pl.ds(r, 1), :] = chain[(at >> 3) + rows, pl.ds(at & 7, 1), :]

    column = code_ref[1, :, pl.ds(pl.multiple_of(group * quarter, 128), quarter)]
    turned = jnp.transpose(picked[...])
    here = lax.broadcasted_iota(jnp.int32, turned.shape, 0) == column
    arrived = jnp.sum(jnp.where(here, turned, 0.0), axis=0, keepdims=True) * spacing
    for k in range(LOW):
        part[k] = arrived[:, k * share : (k + 1) * share]

    for v in range(rows):
        chain_field[slot(span - 2, v)] = jnp.zeros((8, cells_z), jnp.float32)
        chain_field[slot(span - 1, v)] = jnp.zeros((8, cells_z), jnp.float32)
        chain_field[slot(span, v)] = jnp.zeros((8, cells_z), jnp.float32)
        other_field[slot(span, v)] = jnp.zeros((8, cells_z), jnp.float32)

    time_copy.wait_recv()
    bound = jnp.where(upper, grid_x - centre, centre)

    def weigh(at, i, own, theirs, weight, supply, field, tally, turned):
        cur = [theirs[slot(at, v)] for v in range(rows)]
        cut_before = bound == at
        cut_after = bound == at + 1
        for v in range(rows):
            q = (i + 1 + v) % 2
            one = own[slot(at, v)]

            def gain(value):
                return jnp.maximum(value - one, 0.0)

            before = gain(theirs[slot(at - 1, v)])
            after = gain(theirs[slot(at + 1, v)])
            if i % half == 0:
                before = jnp.where(cut_before, 0.0, before)
            if (i + 1) % half == 0:
                after = jnp.where(cut_after, 0.0, after)
            up = gain(y_up(cur, v))
            down = gain(y_down(cur, v))
            if v + 1 == rows:
                up = jnp.where(sub_last, 0.0, up)
            if v == 0:
                down = jnp.where(sub_first, 0.0, down)
            k = q ^ turned
            across = jnp.where(edge_z[k], 0.0, gain(jnp.take_along_axis(cur[v], far[k], axis=1)))
            parts = (before, after, down, up, gain(cur[v]), across)
            total = ((parts[0] + parts[1]) + (parts[2] + parts[3])) + (parts[4] + parts[5])
            inverse = 1.0 / (1.0 + total)
            spot = at * rows + v
            for n, gained in enumerate(parts):
                weight[n, spot] = gained * inverse
            value = (tally_ref[tally, spot] * one - tally_ref[tally + 1, spot]) * inverse
            supply[spot] = value
            if turned:
                field[slot(at, v)] = value

    @pl.loop(0, span // half)
    def _(chunk):
        for i in range(half):
            at = chunk * half + i
            weigh(at, i, twin_time, chain, other_weight, other_supply, other_field, 2, 1)
            weigh(at, i, chain, twin_time, chain_weight, chain_supply, chain_field, 0, 0)

    for v in range(rows):
        other_field[slot(-1, v)] = swing(other_field[slot(0, v)])

    def backward(count, dst, weight, supply, src, turned):
        for i in range(count):
            cur = [src[slot(i, v)] for v in range(rows)]
            for v in range(rows):
                q = (i + 1 + v) % 2
                spot = i * rows + v
                before = src[slot(i - 1, v)] if i else swing(cur[v])
                acc = supply[spot] + weight[0, spot] * before
                acc = acc + weight[1, spot] * src[slot(i + 1, v)]
                side = weight[2, spot] * y_down(cur, v) + weight[3, spot] * y_up(cur, v)
                across = jnp.take_along_axis(cur[v], far[q ^ turned], axis=1)
                acc = (acc + side) + (weight[4, spot] * cur[v] + weight[5, spot] * across)
                dst[slot(i, v)] = acc

    def rounds(first, times):
        count = half + ITERS - first

        @pl.loop(0, times)
        def _(_step):
            backward(count, chain_field, chain_weight, chain_supply, other_field, 0)
            backward(count - 1, other_field, other_weight, other_supply, chain_field, 1)

    rounds(2, 3)
    rounds(8, 2)
    rounds(12, 2)
    backward(half, chain_field, chain_weight, chain_supply, other_field, 0)

    for k in range(LOW):
        for t in range(0, depth, 2):
            low_side = k < LOW // 2
            near, next_to = (
                (half - 1 - (k * depth + t + n)) if low_side else (k * depth + t + n - half) for n in range(2)
            )
            for v in range(rows):
                a = chain_field[slot(near, v)]
                b = chain_field[slot(next_to, v)]
                both = jnp.where(upper, swing(b), a) if low_side else jnp.where(upper, b, swing(a))
                packed[k, t // 2, pl.ds(v, 8, stride=rows), :] = both

    keep = slots_ref.shape[2]

    def ship(k):
        c, b, p = peer(k)
        return remote(
            packed.at[p, :, pl.ds(c * keep, keep)], slots_ref.at[mine], send_sem.at[k], recv_sem.at[mine], c, b
        )

    for k in range(1, peers):
        ship(k).start()
    stay = pltpu.make_async_copy(
        packed.at[place, :, pl.ds(core * keep, keep)], slots_ref.at[mine], self_sem
    )
    stay.start()

    target = core - h + place // 2
    local = lax.rem(place, 2)

    def word(k):
        return remote(
            part.at[k], got_ref.at[local, h], part_send.at[k], part_recv.at[local, h], target, base + k
        )

    def home(k):
        return (target == core) & (place == k)

    for k in range(LOW):
        pl.when(jnp.logical_not(home(k)))(word(k).start)

        @pl.when(home(k))
        def _():
            got_ref[local, h] = part[k]

    def word_in(n, side):
        return remote(
            part.at[0], got_ref.at[n, side], part_send.at[0], part_recv.at[n, side], core, brick
        )

    for n in range(2):
        for side in range(2):
            from_me = (place == 2 * h + n) & (h == side)
            pl.when(jnp.logical_not(from_me))(word_in(n, side).wait_recv)
    for k in range(1, peers):
        m = lax.rem(mine + k, peers)
        remote(
            packed.at[0, :, pl.ds(0, keep)], slots_ref.at[m], send_sem.at[k], recv_sem.at[m], core, brick
        ).wait_recv()
    for k in range(1, peers):
        ship(k).wait_send()
    for k in range(LOW):
        pl.when(jnp.logical_not(home(k)))(word(k).wait_send)
    stay.wait()
    time_copy.wait_send()


def finish_kernel(cores, slots_ref, got_ref, full_ref, out_ref, arr_ref):
    depth, keep, cells_z = out_ref.shape
    half_z = cells_z // 2
    first = lax.axis_index("brick") * depth
    row = pl.multiple_of(lax.axis_index("src") * keep, 8)
    lane = lax.broadcasted_iota(jnp.int32, (8, cells_z), 1)
    sub = lax.broadcasted_iota(jnp.int32, (8, cells_z), 0)
    upper = lane >= half_z
    plain = ((sub + jnp.where(upper, 1, 0)) & 1) == 0
    join = (lane & 1) * half_z + (lane >> 1)
    for t in range(depth // 2):
        for y in range(0, keep, 8):
            sums = []
            for colour in range(2):
                total = None
                for c in range(colour, cores, 2):
                    for k in range(LOW):
                        one = slots_ref[c * LOW + k, t, pl.ds(y, 8), :]
                        total = one if total is None else total + one
                sums.append(total)
            even = jnp.where(plain, sums[0], sums[1])
            odd = jnp.where(plain, sums[1], sums[0])
            moved = pltpu.roll(jnp.where(upper, even, odd), half_z, 1)
            for n, packed in enumerate((jnp.where(upper, moved, even), jnp.where(upper, odd, moved))):
                value = jnp.take_along_axis(packed, join, axis=1)
                slow = full_ref[first + 2 * t + n, pl.ds(row + y, 8), :]
                out_ref[2 * t + n, pl.ds(y, 8), :] = (slow * spacing) * value
    for n in range(2):
        arr_ref[pl.ds(n, 1), :] = got_ref[n, 0] + got_ref[n, 1]


def per_device(slowness, source_x, source_y, source_z, station_x, station_y, station_z, observed):
    bricks = lax.axis_size("brick")
    cores = lax.axis_size("src")
    depth, cells_y, cells_z = slowness.shape
    grid_x = depth * bricks
    rec = station_x.shape[0]
    rows = cells_y // 8
    ring = grid_x // 2
    half = LOW * depth // 2
    span = half + ITERS
    assert source_x.shape[0] == 2 and bricks % LOW == 0 and cores % 2 == 0
    assert half % 2 == 0 and span % half == 0 and span + 1 <= ring and (span * rows * 8) % TALLY == 0
    f32 = jnp.float32
    i32 = jnp.int32

    full, tally, code, spot = pl.pallas_call(
        functools.partial(gather_kernel, bricks),
        name="gather",
        out_shape=(
            jax.ShapeDtypeStruct((grid_x, cells_y, cells_z), f32),
            jax.ShapeDtypeStruct((4, span * rows, 8, cells_z), f32),
            jax.ShapeDtypeStruct((2, 1, rec), i32),
            jax.ShapeDtypeStruct((8, cells_z), i32),
        ),
        in_specs=[HBM] * 8,
        out_specs=(VMEM, VMEM, VMEM, VMEM),
        scratch_shapes=[
            pltpu.VMEM((4 * cells_z, rec), jnp.bfloat16),
            pltpu.SemaphoreType.DMA((2, bricks // LOW)),
            pltpu.SemaphoreType.DMA((3, bricks)),
            pltpu.SemaphoreType.DMA((bricks,)),
            pltpu.SemaphoreType.DMA((bricks,)),
            pltpu.SemaphoreType.DMA,
            pltpu.VMEM((1, rec), i32),
            pltpu.VMEM((1, rec), i32),
            pltpu.VMEM((1, rec), i32),
            pltpu.VMEM(observed.shape, f32),
            pltpu.SMEM((2,), i32),
            pltpu.SMEM((2,), i32),
            pltpu.SMEM((2,), i32),
            pltpu.SemaphoreType.DMA((7,)),
            pltpu.SemaphoreType.DMA((3,)),
            pltpu.SemaphoreType.DMA((3,)),
        ],
        compiler_params=pltpu.CompilerParams(
            collective_id=0, has_side_effects=True, vmem_limit_bytes=GATHER_VMEM
        ),
    )(
        slowness,
        source_x,
        source_y,
        source_z,
        station_x[None],
        station_y[None],
        station_z[None],
        observed,
    )

    share = rec // bricks
    quarter = share * LOW
    keep = cells_y // cores
    layer = (rows, 8, cells_z)
    ring_shape = ((ring + 2) * rows, 8, cells_z)
    slots, got = pl.pallas_call(
        functools.partial(solve_kernel, depth, cores),
        name="solve",
        out_shape=(
            jax.ShapeDtypeStruct((LOW * cores, depth // 2, keep, cells_z), f32),
            jax.ShapeDtypeStruct((2, 2, 1, share), f32),
        ),
        in_specs=[VMEM] * 4,
        out_specs=(VMEM, VMEM),
        scratch_shapes=[
            pltpu.VMEM(ring_shape, f32),
            pltpu.VMEM(ring_shape, f32),
            pltpu.VMEM((ring * rows, 8, cells_z), f32),
            pltpu.VMEM((ring * rows, 8, cells_z), f32),
            pltpu.VMEM(((span + 2) * rows, 8, cells_z), f32),
            pltpu.VMEM((6, span * rows, 8, cells_z), f32),
            pltpu.VMEM((6, span * rows, 8, cells_z), f32),
            pltpu.VMEM((span * rows, 8, cells_z), f32),
            pltpu.VMEM((span * rows, 8, cells_z), f32),
            pltpu.VMEM(((span + 2) * rows, 8, cells_z), f32),
            pltpu.VMEM(((span + 2) * rows, 8, cells_z), f32),
            pltpu.VMEM((LOW, depth // 2, cells_y, cells_z), f32),
            pltpu.VMEM((quarter, cells_z), f32),
            pltpu.VMEM((LOW, 1, share), f32),
            pltpu.SMEM((1, rec), i32),
            pltpu.SemaphoreType.DMA,
            pltpu.SemaphoreType.DMA,
            pltpu.SemaphoreType.DMA,
            pltpu.SemaphoreType.DMA((LOW * cores,)),
            pltpu.SemaphoreType.DMA((LOW * cores,)),
            pltpu.SemaphoreType.DMA((LOW,)),
            pltpu.SemaphoreType.DMA((2, 2)),
            pltpu.SemaphoreType.DMA,
        ],
        compiler_params=pltpu.CompilerParams(
            collective_id=1, has_side_effects=True, vmem_limit_bytes=SOLVE_VMEM
        ),
    )(code, spot, full, tally)

    return tuple(
        pl.pallas_call(
            functools.partial(finish_kernel, cores),
            name="finish",
            out_shape=(
                jax.ShapeDtypeStruct((depth, keep, cells_z), f32),
                jax.ShapeDtypeStruct((2, share), f32),
            ),
            in_specs=[VMEM] * 3,
            compiler_params=pltpu.CompilerParams(vmem_limit_bytes=FINISH_VMEM),
        )(slots, got, full)
    )


def solution(mesh):
    in_specs = (P("brick", None, None), P("src"), P("src"), P("src"), P(), P(), P(), P("src", None))
    out_specs = (P("brick", "src", None), P("src", "brick"))
    return jax.shard_map(
        per_device, mesh=mesh, in_specs=in_specs, out_specs=out_specs, check_vma=False
    )
```

time: 80.4 us -> 56.9 us (0.71)
  Pallas kernels: 70.1 us -> 50.1 us
  local copies, waits for them, and re-layouts: 8.32 us -> 5.67 us
    pallas_call x3, Pallas kernels: 70.1 us -> 50.1 us  [the longest x1 25.3 us: per_device(): pl.pallas_call(functools.partial(solve_kernel, depth, cores), name='solve...]
    unnamed x25 -> x16, local copies, waits for them, and re-layouts: 8.32 us -> 5.67 us
where the time goes in v1:
time: 56.9 us; the launch traced here: 56.4 us
  Pallas kernels  50.1 us (88%)
  local copies, waits for them, and re-layouts  5.67 us (10%)
  between operations  0.66 us (1%)
    pallas_call x1, Pallas kernels, per_device(): pl.pallas_call(functools.partial(solve_kernel, depth, cores), name='solve...  25.3 us
    pallas_call x1, Pallas kernels, per_device(): pl.pallas_call(functools.partial(gather_kernel, bricks), name='gather', o...  24 us
    unnamed x16, local copies, waits for them, and re-layouts  5.67 us

profile of v1, /device:TPU:0, one launch (start us, length us, event | category | flops | bytes accessed | tf_op | source)
XLA Modules:
  0.0 56.4 jit_solution(15013605363283878202)
XLA Ops:
  0.6 0.0 copy-start
  0.6 0.9 %copy-done = f32[4,64,128]{2,1,0:T(8,128)S(1)} copy-done((f32[4,64,128]{2,1,0:T(8,128)S(1)}, f32[4,64,128]{2,1,0:T(8,128)}, u32[]{:S(2)}) %copy-start) | copy-done | bytes 131096
  1.5 0.0 copy-start.1
  1.5 0.7 %copy-done.1 = f32[2,2048]{1,0:T(2,128)S(1)} copy-done((f32[2,2048]{1,0:T(2,128)S(1)}, f32[2,2048]{1,0:T(2,128)}, u32[]{:S(2)}) %copy-start.1) | copy-done | bytes 16408
  2.3 0.0 copy-start.2
  2.3 0.7 %copy-done.2 = s32[2048]{0:T(1024)S(1)} copy-done((s32[2048]{0:T(1024)S(1)}, s32[2048]{0:T(1024)}, u32[]{:S(2)}) %copy-start.2) | copy-done | bytes 8216
  3.0 0.0 copy-start.3
  3.0 0.7 %copy-done.3 = s32[2048]{0:T(1024)S(1)} copy-done((s32[2048]{0:T(1024)S(1)}, s32[2048]{0:T(1024)}, u32[]{:S(2)}) %copy-start.3) | copy-done | bytes 8216
  3.7 0.0 copy-start.4
  3.7 0.7 %copy-done.4 = s32[2048]{0:T(1024)S(1)} copy-done((s32[2048]{0:T(1024)S(1)}, s32[2048]{0:T(1024)}, u32[]{:S(2)}) %copy-start.4) | copy-done | bytes 8216
  4.3 0.0 copy-start.5
  4.3 0.7 %copy-done.5 = s32[2]{0:T(128)S(1)} copy-done((s32[2]{0:T(128)S(1)}, s32[2]{0:T(128)}, u32[]{:S(2)}) %copy-start.5) | copy-done | bytes 32
  5.0 0.0 copy-start.6
  5.0 0.7 %copy-done.6 = s32[2]{0:T(128)S(1)} copy-done((s32[2]{0:T(128)S(1)}, s32[2]{0:T(128)}, u32[]{:S(2)}) %copy-start.6) | copy-done | bytes 32
  5.7 0.0 copy-start.7
  5.7 0.7 %copy-done.7 = s32[2]{0:T(128)S(1)} copy-done((s32[2]{0:T(128)S(1)}, s32[2]{0:T(128)}, u32[]{:S(2)}) %copy-start.7) | copy-done | bytes 32
  6.3 24.0 %gather.1 = (f32[64,64,128]{2,1,0:T(8,128)S(1)}, f32[4,192,8,128]{3,2,1,0:T(8,128)S(1)}, s32[2,1,2048]{2,1,0:T(1,128)S(1)}, s32[8,128]{1,0:T(8,128)S(1)}) custom-call(f32[4,64,128]{2,1,0:T(8,128)S(1)} %copy-done, s32[2]{0:T(128)S(1)} %copy-done.5, s32[2]{0:T(128)S(1)} %copy-done.6, s32[2]{0:T(128)S(1)} %copy-done.7, s32[1,2048]{1,0:T(1,128)S(1)} %bitcast.3, ...), custom_call_target="tpu_custom_call" | custom-call | tf_op jit(solution)/shard_map/gather/pallas_call | solution.py:690
  30.3 25.3 %solve.1 = (f32[8,2,32,128]{3,2,1,0:T(8,128)S(1)}, f32[2,2,1,128]{3,2,1,0:T(1,128)S(1)}) custom-call(s32[2,1,2048]{2,1,0:T(1,128)S(1)} %get-tuple-element.8.code_ref, s32[8,128]{1,0:T(8,128)S(1)} %get-tuple-element.9.spot_ref, f32[64,64,128]{2,1,0:T(8,128)S(1)} %get-tuple-element.10.full_ref, f32[4,192,8,128]{3,2,1,0:T(8,128)S(1)} %get-tuple-element.11.tally_ref), custom_call_target="tpu_custom_call" | custom-call | tf_op jit(solution)/shard_map/solve/pallas_call | solution.py:738
  55.7 0.8 %finish.1 = (f32[4,32,128]{2,1,0:T(8,128)}, f32[2,128]{1,0:T(2,128)}) custom-call(f32[8,2,32,128]{3,2,1,0:T(8,128)S(1)} %get-tuple-element.12.slots_ref, f32[2,2,1,128]{3,2,1,0:T(1,128)S(1)} %get-tuple-element.13.got_ref, f32[64,64,128]{2,1,0:T(8,128)S(1)} %get-tuple-element.10.full_ref), custom_call_target="tpu_custom_call" | custom-call | tf_op jit(solution)/shard_map/finish/pallas_call | solution.py:778
Async XLA Ops:
  0.6 0.9 %copy-start = (f32[4,64,128]{2,1,0:T(8,128)S(1)}, f32[4,64,128]{2,1,0:T(8,128)}, u32[]{:S(2)}) copy-start(f32[4,64,128]{2,1,0:T(8,128)} %slow_ref.1) | copy-start | bytes 393220
  1.5 0.7 %copy-start.1 = (f32[2,2048]{1,0:T(2,128)S(1)}, f32[2,2048]{1,0:T(2,128)}, u32[]{:S(2)}) copy-start(f32[2,2048]{1,0:T(2,128)} %obs_ref.1) | copy-start | bytes 49156
  2.3 0.7 %copy-start.2 = (s32[2048]{0:T(1024)S(1)}, s32[2048]{0:T(1024)}, u32[]{:S(2)}) copy-start(s32[2048]{0:T(1024)} %param.12) | copy-start | bytes 24580
  3.0 0.7 %copy-start.3 = (s32[2048]{0:T(1024)S(1)}, s32[2048]{0:T(1024)}, u32[]{:S(2)}) copy-start(s32[2048]{0:T(1024)} %param.13) | copy-start | bytes 24580
  3.7 0.7 %copy-start.4 = (s32[2048]{0:T(1024)S(1)}, s32[2048]{0:T(1024)}, u32[]{:S(2)}) copy-start(s32[2048]{0:T(1024)} %param.14) | copy-start | bytes 24580
  4.3 0.7 %copy-start.5 = (s32[2]{0:T(128)S(1)}, s32[2]{0:T(128)}, u32[]{:S(2)}) copy-start(s32[2]{0:T(128)} %sx_ref.1) | copy-start | bytes 28
  5.0 0.7 %copy-start.6 = (s32[2]{0:T(128)S(1)}, s32[2]{0:T(128)}, u32[]{:S(2)}) copy-start(s32[2]{0:T(128)} %sy_ref.1) | copy-start | bytes 28
  5.7 0.7 %copy-start.7 = (s32[2]{0:T(128)S(1)}, s32[2]{0:T(128)}, u32[]{:S(2)}) copy-start(s32[2]{0:T(128)} %sz_ref.1) | copy-start | bytes 28

commit v2 on v1

--- a/solution.py
+++ b/solution.py
@@ -149,14 +149,6 @@
     seen_send = remote(obs_ref, seen_buf, word_send.at[0], word_recv.at[0], twin, me)
     spot_send = remote(spot_ref, spot_ref, word_send.at[1], word_recv.at[1], twin, me)
 
-    pl.semaphore_wait(barrier, lines + 2)
-    pl.when(owner)(seen_send.start)
-    for k in range(1, lines):
-        own_line(k, False)
-        if k == 1:
-            sends(me, True, False)
-    own_copy.start()
-
     def arrived(q):
         remote(piece(q, h), piece(q, h), send_sem.at[0, q], recv_sem.at[q], core, first).wait_recv()
 
@@ -228,11 +220,19 @@
     upper = away < ring
     step_x = jnp.where(upper, away, grid_x - 1 - away)
     row = (step_x * rows + (sty & (rows - 1))) * 8 + (sty >> shift)
-    column = jnp.where(upper, cells_z // 2, 0) + (stz >> 1)
+    column = jnp.where(upper, cells_z - 1 - (stz >> 1), stz >> 1)
     column = jnp.where(((stx + sty + stz) & 1) == h, column, -1)
     code_ref[0] = row
     code_ref[1] = column
     rec = row.shape[1]
+    pl.semaphore_wait(barrier, lines + 2)
+    pl.when(owner)(seen_send.start)
+    for k in range(1, lines):
+        own_line(k, False)
+        if k == 1:
+            sends(me, True, False)
+    own_copy.start()
+
     hit = lax.broadcasted_iota(jnp.int32, (cells_z, rec), 0) == column
 
     pl.when(owner)(seen_copy.wait)
@@ -269,8 +269,8 @@
 
     @pl.loop(0, max(rounds, blocks + 1))
     def _(step):
+        pl.when(step < rounds)(lambda: turn(step + 1, False))
         pl.when(step < blocks)(lambda: tally(step))
-        pl.when(step < rounds)(lambda: turn(step + 1, False))
         pl.when(step == blocks)(tally_send.start)
 
     own_copy.wait()
@@ -369,13 +369,13 @@
     sub_first = sub == 0
     sub_last = sub == 7
     upper = lane >= half_z
-    inner = jnp.where(upper, lane - half_z, lane)
+    inner = jnp.where(upper, cells_z - 1 - lane, lane)
     parity = [lax.rem(q + h, 2) for q in range(2)]
     cell_z = [inner * 2 + jnp.where(upper, 1 - p, p) for p in parity]
     from_low = [(lane & 1) == p for p in parity]
-    slide = [inner + jnp.where(upper, 1, -1) * (1 - 2 * p) for p in parity]
-    edge_z = [(s < 0) | (s >= half_z) for s in slide]
-    far = [jnp.where(upper, half_z, 0) + jnp.clip(s, 0, half_z - 1) for s in slide]
+    edge_z = [(lane & (half_z - 1)) == p * (half_z - 1) for p in parity]
+    slide = [1 + p * (cells_z - 2) for p in parity]
+    mirror = cells_z - 1 - lane
 
     def slot(i, v):
         return (i + 1) * rows + v
@@ -406,10 +406,11 @@
                 q = (j + 1 + v) % 2
                 low = full_ref[x_low, pl.ds(v, 8, stride=rows), :]
                 high = full_ref[x_high, pl.ds(v, 8, stride=rows), :]
-                for field, cost, k, natural in (
+                pair_of = (
                     (chain, chain_cost, q, jnp.where(from_low[q], low, high)),
                     (other, other_cost, 1 - q, jnp.where(from_low[q], high, low)),
-                ):
+                )
+                for field, cost, k, natural in pair_of if q else pair_of[::-1]:
                     slow = jnp.take_along_axis(natural, cell_z[k], axis=1)
                     square = dx + flat[k * rows + v]
                     start = square * lax.rsqrt(jnp.maximum(square, unit * 0.5))
@@ -421,21 +422,29 @@
     }
 
     def swing(one):
-        return pltpu.roll(one, half_z, 1)
+        return jnp.take_along_axis(one, mirror, axis=1)
+
+    def across_z(one, k):
+        return pltpu.roll(one, slide[k], 1)
 
     def y_up(cur, v):
         return cur[v + 1] if v + 1 < rows else pltpu.roll(cur[0], 7, 0)
 
     def y_down(cur, v):
         return cur[v - 1] if v else pltpu.roll(cur[rows - 1], 1, 0)
+
+    def order(i):
+        return [v ^ (i & 1) for v in range(rows)]
 
     def sweep(dst, cost, src, turned):
         for i in range(ring):
             cur = [src[slot(i, v)] for v in range(rows)]
-            for v in range(rows):
+            if i == 0 or i + 1 == ring:
+                swung = [swing(one) for one in cur]
+            for v in order(i + turned):
                 q = (i + 1 + v) % 2
-                before = src[slot(i - 1, v)] if i else swing(cur[v])
-                after = src[slot(i + 1, v)] if i + 1 < ring else swing(cur[v])
+                before = src[slot(i - 1, v)] if i else swung[v]
+                after = src[slot(i + 1, v)] if i + 1 < ring else swung[v]
                 if i in cuts:
                     before = jnp.where(cuts[i], big_value, before)
                 if i + 1 in cuts:
@@ -446,7 +455,8 @@
                     up = jnp.where(sub_last, big_value, up)
                 if v == 0:
                     down = jnp.where(sub_first, big_value, down)
-                across = jnp.take_along_axis(cur[v], far[q ^ turned], axis=1)
+                k = q ^ turned
+                across = jnp.where(edge_z[k], cur[v], across_z(cur[v], k))
                 low = jnp.minimum(
                     jnp.minimum(jnp.minimum(before, after), jnp.minimum(up, down)),
                     jnp.minimum(cur[v], across),
@@ -505,7 +515,7 @@
         cur = [theirs[slot(at, v)] for v in range(rows)]
         cut_before = bound == at
         cut_after = bound == at + 1
-        for v in range(rows):
+        for v in order(i + turned):
             q = (i + 1 + v) % 2
             one = own[slot(at, v)]
 
@@ -525,7 +535,7 @@
             if v == 0:
                 down = jnp.where(sub_first, 0.0, down)
             k = q ^ turned
-            across = jnp.where(edge_z[k], 0.0, gain(jnp.take_along_axis(cur[v], far[k], axis=1)))
+            across = jnp.where(edge_z[k], 0.0, gain(across_z(cur[v], k)))
             parts = (before, after, down, up, gain(cur[v]), across)
             total = ((parts[0] + parts[1]) + (parts[2] + parts[3])) + (parts[4] + parts[5])
             inverse = 1.0 / (1.0 + total)
@@ -550,14 +560,16 @@
     def backward(count, dst, weight, supply, src, turned):
         for i in range(count):
             cur = [src[slot(i, v)] for v in range(rows)]
-            for v in range(rows):
+            if i == 0:
+                swung = [swing(one) for one in cur]
+            for v in order(i + turned):
                 q = (i + 1 + v) % 2
                 spot = i * rows + v
-                before = src[slot(i - 1, v)] if i else swing(cur[v])
+                before = src[slot(i - 1, v)] if i else swung[v]
                 acc = supply[spot] + weight[0, spot] * before
                 acc = acc + weight[1, spot] * src[slot(i + 1, v)]
                 side = weight[2, spot] * y_down(cur, v) + weight[3, spot] * y_up(cur, v)
-                across = jnp.take_along_axis(cur[v], far[q ^ turned], axis=1)
+                across = across_z(cur[v], q ^ turned)
                 acc = (acc + side) + (weight[4, spot] * cur[v] + weight[5, spot] * across)
                 dst[slot(i, v)] = acc
 
@@ -650,7 +662,8 @@
     sub = lax.broadcasted_iota(jnp.int32, (8, cells_z), 0)
     upper = lane >= half_z
     plain = ((sub + jnp.where(upper, 1, 0)) & 1) == 0
-    join = (lane & 1) * half_z + (lane >> 1)
+    join = jnp.where((lane & 1) == 0, lane >> 1, cells_z - 1 - (lane >> 1))
+    mirror = cells_z - 1 - lane
     for t in range(depth // 2):
         for y in range(0, keep, 8):
             sums = []
@@ -663,7 +676,7 @@
                 sums.append(total)
             even = jnp.where(plain, sums[0], sums[1])
             odd = jnp.where(plain, sums[1], sums[0])
-            moved = pltpu.roll(jnp.where(upper, even, odd), half_z, 1)
+            moved = jnp.take_along_axis(jnp.where(upper, even, odd), mirror, axis=1)
             for n, packed in enumerate((jnp.where(upper, moved, even), jnp.where(upper, odd, moved))):
                 value = jnp.take_along_axis(packed, join, axis=1)
                 slow = full_ref[first + 2 * t + n, pl.ds(row + y, 8), :]
@@ -720,14 +733,19 @@
             collective_id=0, has_side_effects=True, vmem_limit_bytes=GATHER_VMEM
         ),
     )(
-        slowness,
-        source_x,
-        source_y,
-        source_z,
-        station_x[None],
-        station_y[None],
-        station_z[None],
-        observed,
+        *(
+            pltpu.with_memory_space_constraint(a, pltpu.HBM)
+            for a in (
+                slowness,
+                source_x,
+                source_y,
+                source_z,
+                station_x[None],
+                station_y[None],
+                station_z[None],
+                observed,
+            )
+        )
     )
 
     share = rec // bricks

time: 56.9 us -> 48.8 us (0.86)
  local copies, waits for them, and re-layouts: 5.67 us -> 0 us
  Pallas kernels: 50.1 us -> 48 us
    unnamed x16 -> x0, local copies, waits for them, and re-layouts: 5.67 us -> none
    pallas_call x1, Pallas kernels: 25.3 us -> 23 us  [per_device(): pl.pallas_call(functools.partial(solve_kernel, depth, cores), name='solve...]
where the time goes in v2:
time: 48.8 us; the launch traced here: 48.6 us
  Pallas kernels  48 us (98%)
  between operations  0.65 us (1%)
    pallas_call x1, Pallas kernels, per_device(): pl.pallas_call(functools.partial(gather_kernel, bricks), name='gather', o...  24.1 us
    pallas_call x1, Pallas kernels, per_device(): pl.pallas_call(functools.partial(solve_kernel, depth, cores), name='solve...  23 us

profile of v2, /device:TPU:0, one launch (start us, length us, event | category | flops | bytes accessed | tf_op | source)
XLA Modules:
  0.0 48.6 jit_solution(14165838466801041908)
XLA Ops:
  0.6 24.1 %gather.1 = (f32[64,64,128]{2,1,0:T(8,128)S(1)}, f32[4,192,8,128]{3,2,1,0:T(8,128)S(1)}, s32[2,1,2048]{2,1,0:T(1,128)S(1)}, s32[8,128]{1,0:T(8,128)S(1)}) custom-call(f32[4,64,128]{2,1,0:T(8,128)} %slow_ref.1, s32[2]{0:T(128)} %sx_ref.1, s32[2]{0:T(128)} %sy_ref.1, s32[2]{0:T(128)} %sz_ref.1, s32[1,2048]{1,0:T(1,128)} %bitcast.3, s32[1,2048]{1,0:T(1,128)} %bitcast.4, ...), custom_call_target="tpu_custom_call" | custom-call | tf_op jit(solution)/shard_map/gather/pallas_call | solution.py:703
  24.8 23.0 %solve.1 = (f32[8,2,32,128]{3,2,1,0:T(8,128)S(1)}, f32[2,2,1,128]{3,2,1,0:T(1,128)S(1)}) custom-call(s32[2,1,2048]{2,1,0:T(1,128)S(1)} %get-tuple-element.8.code_ref, s32[8,128]{1,0:T(8,128)S(1)} %get-tuple-element.9.spot_ref, f32[64,64,128]{2,1,0:T(8,128)S(1)} %get-tuple-element.10.full_ref, f32[4,192,8,128]{3,2,1,0:T(8,128)S(1)} %get-tuple-element.11.tally_ref), custom_call_target="tpu_custom_call" | custom-call | tf_op jit(solution)/shard_map/solve/pallas_call | solution.py:756
  47.8 0.8 %finish.1 = (f32[4,32,128]{2,1,0:T(8,128)}, f32[2,128]{1,0:T(2,128)}) custom-call(f32[8,2,32,128]{3,2,1,0:T(8,128)S(1)} %get-tuple-element.12.slots_ref, f32[2,2,1,128]{3,2,1,0:T(1,128)S(1)} %get-tuple-element.13.got_ref, f32[64,64,128]{2,1,0:T(8,128)S(1)} %get-tuple-element.10.full_ref), custom_call_target="tpu_custom_call" | custom-call | tf_op jit(solution)/shard_map/finish/pallas_call | solution.py:796

commit v3 on v2

--- a/solution.py
+++ b/solution.py
@@ -149,6 +149,14 @@
     seen_send = remote(obs_ref, seen_buf, word_send.at[0], word_recv.at[0], twin, me)
     spot_send = remote(spot_ref, spot_ref, word_send.at[1], word_recv.at[1], twin, me)
 
+    pl.semaphore_wait(barrier, lines + 2)
+    pl.when(owner)(seen_send.start)
+    for k in range(1, lines):
+        own_line(k, False)
+        if k == 1:
+            sends(me, True, False)
+    own_copy.start()
+
     def arrived(q):
         remote(piece(q, h), piece(q, h), send_sem.at[0, q], recv_sem.at[q], core, first).wait_recv()
 
@@ -225,14 +233,6 @@
     code_ref[0] = row
     code_ref[1] = column
     rec = row.shape[1]
-    pl.semaphore_wait(barrier, lines + 2)
-    pl.when(owner)(seen_send.start)
-    for k in range(1, lines):
-        own_line(k, False)
-        if k == 1:
-            sends(me, True, False)
-    own_copy.start()
-
     hit = lax.broadcasted_iota(jnp.int32, (cells_z, rec), 0) == column
 
     pl.when(owner)(seen_copy.wait)
@@ -392,10 +392,10 @@
             dy = (sub * rows + v - sy).astype(jnp.float32)
             flat.append((dy * dy + dz) * unit)
 
-    @pl.loop(0, ring // 2)
-    def _(pair):
-        for j in range(2):
-            i = pair * 2 + j
+    @pl.loop(0, ring // 4)
+    def _(quad):
+        for j in range(4):
+            i = quad * 4 + j
             x_low = centre - 1 - i
             x_low = jnp.where(x_low < 0, x_low + grid_x, x_low)
             x_high = centre + i
@@ -433,18 +433,18 @@
     def y_down(cur, v):
         return cur[v - 1] if v else pltpu.roll(cur[rows - 1], 1, 0)
 
-    def order(i):
-        return [v ^ (i & 1) for v in range(rows)]
+    def layer_of(ref, i):
+        return [ref[slot(i, v)] for v in range(rows)]
 
     def sweep(dst, cost, src, turned):
+        cur = layer_of(src, 0)
+        prev = [swing(one) for one in cur]
         for i in range(ring):
-            cur = [src[slot(i, v)] for v in range(rows)]
-            if i == 0 or i + 1 == ring:
-                swung = [swing(one) for one in cur]
-            for v in order(i + turned):
+            after_of = layer_of(src, i + 1) if i + 1 < ring else [swing(one) for one in cur]
+            for v in range(rows):
                 q = (i + 1 + v) % 2
-                before = src[slot(i - 1, v)] if i else swung[v]
-                after = src[slot(i + 1, v)] if i + 1 < ring else swung[v]
+                before = prev[v]
+                after = after_of[v]
                 if i in cuts:
                     before = jnp.where(cuts[i], big_value, before)
                 if i + 1 in cuts:
@@ -457,11 +457,11 @@
                     down = jnp.where(sub_first, big_value, down)
                 k = q ^ turned
                 across = jnp.where(edge_z[k], cur[v], across_z(cur[v], k))
-                low = jnp.minimum(
-                    jnp.minimum(jnp.minimum(before, after), jnp.minimum(up, down)),
-                    jnp.minimum(cur[v], across),
-                )
+                low = jnp.minimum(across, cur[v])
+                for value in (before, after, down, up):
+                    low = jnp.minimum(low, value)
                 dst[slot(i, v)] = jnp.minimum(dst[slot(i, v)], low + cost[i * rows + v])
+            prev, cur = cur, after_of
 
     assert ITERS % 2 == 0
 
@@ -479,11 +479,15 @@
         chain[slot(-1, v)] = swing(chain[slot(0, v)])
 
     pl.semaphore_wait(barrier, peers - 1)
-    reach = span + 2
-    time_copy = remote(
-        chain.at[pl.ds(0, reach * rows)], twin_time, time_send, time_recv, twin, brick
-    )
-    time_copy.start()
+    stops = [0] + [(2 + n * half) * rows for n in range(1, span // half + 1)]
+    time_copies = []
+    for n, (low, high) in enumerate(zip(stops, stops[1:])):
+        part_of = pl.ds(low, high - low)
+        time_copies.append(
+            remote(chain.at[part_of], twin_time.at[part_of], time_send.at[n], time_recv.at[n], twin, brick)
+        )
+    for copy in time_copies:
+        copy.start()
 
     load_code.wait()
     unroll = 16
@@ -508,14 +512,13 @@
         chain_field[slot(span, v)] = jnp.zeros((8, cells_z), jnp.float32)
         other_field[slot(span, v)] = jnp.zeros((8, cells_z), jnp.float32)
 
-    time_copy.wait_recv()
     bound = jnp.where(upper, grid_x - centre, centre)
 
     def weigh(at, i, own, theirs, weight, supply, field, tally, turned):
         cur = [theirs[slot(at, v)] for v in range(rows)]
         cut_before = bound == at
         cut_after = bound == at + 1
-        for v in order(i + turned):
+        for v in range(rows):
             q = (i + 1 + v) % 2
             one = own[slot(at, v)]
 
@@ -549,6 +552,8 @@
 
     @pl.loop(0, span // half)
     def _(chunk):
+        for n, copy in enumerate(time_copies):
+            pl.when(chunk == n)(copy.wait_recv)
         for i in range(half):
             at = chunk * half + i
             weigh(at, i, twin_time, chain, other_weight, other_supply, other_field, 2, 1)
@@ -558,20 +563,20 @@
         other_field[slot(-1, v)] = swing(other_field[slot(0, v)])
 
     def backward(count, dst, weight, supply, src, turned):
+        cur = layer_of(src, 0)
+        prev = [swing(one) for one in cur]
         for i in range(count):
-            cur = [src[slot(i, v)] for v in range(rows)]
-            if i == 0:
-                swung = [swing(one) for one in cur]
-            for v in order(i + turned):
+            after_of = layer_of(src, i + 1)
+            for v in range(rows):
                 q = (i + 1 + v) % 2
                 spot = i * rows + v
-                before = src[slot(i - 1, v)] if i else swung[v]
-                acc = supply[spot] + weight[0, spot] * before
-                acc = acc + weight[1, spot] * src[slot(i + 1, v)]
+                acc = supply[spot] + weight[0, spot] * prev[v]
+                acc = acc + weight[1, spot] * after_of[v]
                 side = weight[2, spot] * y_down(cur, v) + weight[3, spot] * y_up(cur, v)
                 across = across_z(cur[v], q ^ turned)
                 acc = (acc + side) + (weight[4, spot] * cur[v] + weight[5, spot] * across)
                 dst[slot(i, v)] = acc
+            prev, cur = cur, after_of
 
     def rounds(first, times):
         count = half + ITERS - first
@@ -650,7 +655,8 @@
     for k in range(LOW):
         pl.when(jnp.logical_not(home(k)))(word(k).wait_send)
     stay.wait()
-    time_copy.wait_send()
+    for copy in time_copies:
+        copy.wait_send()
 
 
 def finish_kernel(cores, slots_ref, got_ref, full_ref, out_ref, arr_ref):
@@ -779,8 +785,8 @@
             pltpu.VMEM((LOW, 1, share), f32),
             pltpu.SMEM((1, rec), i32),
             pltpu.SemaphoreType.DMA,
-            pltpu.SemaphoreType.DMA,
-            pltpu.SemaphoreType.DMA,
+            pltpu.SemaphoreType.DMA((span // half,)),
+            pltpu.SemaphoreType.DMA((span // half,)),
             pltpu.SemaphoreType.DMA((LOW * cores,)),
             pltpu.SemaphoreType.DMA((LOW * cores,)),
             pltpu.SemaphoreType.DMA((LOW,)),

time: 48.8 us -> 45.4 us (0.930)
  Pallas kernels: 48 us -> 44.6 us
    pallas_call x1, Pallas kernels: 23 us -> 19.7 us  [per_device(): pl.pallas_call(functools.partial(solve_kernel, depth, cores), name='solve...]
where the time goes in v3:
time: 45.4 us; the launch traced here: 45.3 us
  Pallas kernels  44.6 us (98%)
  between operations  0.65 us (1%)
    pallas_call x1, Pallas kernels, per_device(): pl.pallas_call(functools.partial(gather_kernel, bricks), name='gather', o...  24.1 us
    pallas_call x1, Pallas kernels, per_device(): pl.pallas_call(functools.partial(solve_kernel, depth, cores), name='solve...  19.7 us

profile of v3, /device:TPU:0, one launch (start us, length us, event | category | flops | bytes accessed | tf_op | source)
XLA Modules:
  0.0 45.3 jit_solution(3125123246522901952)
XLA Ops:
  0.6 24.1 %gather.1 = (f32[64,64,128]{2,1,0:T(8,128)S(1)}, f32[4,192,8,128]{3,2,1,0:T(8,128)S(1)}, s32[2,1,2048]{2,1,0:T(1,128)S(1)}, s32[8,128]{1,0:T(8,128)S(1)}) custom-call(f32[4,64,128]{2,1,0:T(8,128)} %slow_ref.1, s32[2]{0:T(128)} %sx_ref.1, s32[2]{0:T(128)} %sy_ref.1, s32[2]{0:T(128)} %sz_ref.1, s32[1,2048]{1,0:T(1,128)} %bitcast.3, s32[1,2048]{1,0:T(1,128)} %bitcast.4, ...), custom_call_target="tpu_custom_call" | custom-call | tf_op jit(solution)/shard_map/gather/pallas_call | solution.py:709
  24.7 19.7 %solve.1 = (f32[8,2,32,128]{3,2,1,0:T(8,128)S(1)}, f32[2,2,1,128]{3,2,1,0:T(1,128)S(1)}) custom-call(s32[2,1,2048]{2,1,0:T(1,128)S(1)} %get-tuple-element.8.code_ref, s32[8,128]{1,0:T(8,128)S(1)} %get-tuple-element.9.spot_ref, f32[64,64,128]{2,1,0:T(8,128)S(1)} %get-tuple-element.10.full_ref, f32[4,192,8,128]{3,2,1,0:T(8,128)S(1)} %get-tuple-element.11.tally_ref), custom_call_target="tpu_custom_call" | custom-call | tf_op jit(solution)/shard_map/solve/pallas_call | solution.py:762
  44.5 0.8 %finish.1 = (f32[4,32,128]{2,1,0:T(8,128)}, f32[2,128]{1,0:T(2,128)}) custom-call(f32[8,2,32,128]{3,2,1,0:T(8,128)S(1)} %get-tuple-element.12.slots_ref, f32[2,2,1,128]{3,2,1,0:T(1,128)S(1)} %get-tuple-element.13.got_ref, f32[64,64,128]{2,1,0:T(8,128)S(1)} %get-tuple-element.10.full_ref), custom_call_target="tpu_custom_call" | custom-call | tf_op jit(solution)/shard_map/finish/pallas_call | solution.py:802

commit v4 on v3

v4 whole, which is shorter than its diff:
```python
import functools

import jax
import jax.numpy as jnp
from jax import lax
from jax.experimental import pallas as pl
from jax.experimental.pallas import tpu as pltpu
from jax.sharding import PartitionSpec as P

ITERS = 16

spacing = 0.015625
big_value = 1000000.0
start_slowness = 2.0
half_step = 0.5 * spacing
LOW = 4
SOLVE_VMEM = 40 << 20
FINISH_VMEM = 8 << 20
TALLY = 512
REACH = 2

VMEM = pl.BlockSpec(memory_space=pltpu.VMEM)
SMEM = pl.BlockSpec(memory_space=pltpu.SMEM)
HBM = pl.BlockSpec(memory_space=pltpu.HBM)
MESH = pl.DeviceIdType.MESH


def remote(src, dst, send_sem, recv_sem, core, brick):
    return pltpu.make_async_remote_copy(
        src_ref=src,
        dst_ref=dst,
        send_sem=send_sem,
        recv_sem=recv_sem,
        device_id={"src": core, "brick": brick},
        device_id_type=MESH,
    )


def solve_kernel(
    bricks,
    cores,
    slow_ref,
    sx_ref,
    sy_ref,
    sz_ref,
    stx_ref,
    sty_ref,
    stz_ref,
    obs_ref,
    slots_ref,
    got_ref,
    own_ref,
    full_ref,
    tally_ref,
    code_ref,
    spot_ref,
    table,
    chain,
    other,
    chain_cost,
    other_cost,
    twin_time,
    chain_weight,
    other_weight,
    chain_supply,
    other_supply,
    chain_field,
    other_field,
    packed,
    picked,
    part,
    stx_buf,
    sty_buf,
    stz_buf,
    seen_buf,
    code,
    sx_buf,
    sy_buf,
    sz_buf,
    line_sem,
    brick_send,
    brick_recv,
    twin_sem,
    own_sem,
    in_sem,
    word_send,
    word_recv,
    code_sem,
    time_send,
    time_recv,
    send_sem,
    recv_sem,
    part_send,
    part_recv,
    self_sem,
):
    grid_x, cells_y, cells_z = full_ref.shape
    depth = slow_ref.shape[0]
    half_depth = depth // 2
    lines = bricks // LOW
    reach = REACH if lines == REACH + 2 else lines - 1
    early = reach < lines - 1
    rows = cells_y // 8
    shift = rows.bit_length() - 1
    ring = grid_x // 2
    block = LOW * depth
    half = block // 2
    span = half + ITERS
    half_z = cells_z // 2
    me = lax.axis_index("brick")
    core = lax.axis_index("src")
    h = lax.rem(core, 2)
    twin = core + 1 - 2 * h
    line = me // LOW
    place = lax.rem(me, LOW)
    base = line * LOW
    peers = LOW * cores
    mine = core * LOW + place
    centre = line * block + half
    bit_x = lax.rem(me, 2)
    bit_y = lax.rem(me // 2, 2)
    flip_x = 1 - 2 * bit_x
    flip_y = 2 - 4 * bit_y
    first = me + flip_x * (1 - h) + flip_y * h
    second = me + flip_y * (1 - h) + flip_x * h
    corner = me + flip_x + flip_y
    owner = place // 2 == h
    local = lax.rem(place, 2)

    barrier = pltpu.get_barrier_semaphore()

    def greet(c, b):
        pl.semaphore_signal(barrier, inc=1, device_id={"src": c, "brick": b}, device_id_type=MESH)

    def peer(k):
        t = lax.rem(mine + k, peers)
        return t // LOW, base + lax.rem(t, LOW), lax.rem(t, LOW)

    for k in range(1, peers):
        c, b, _ = peer(k)
        greet(c, b)
    for k in range(1, reach + 1):
        pl.when(line >= k)(lambda k=k: greet(core, me - LOW * k))
        pl.when(line + k < lines)(lambda k=k: greet(core, me + LOW * k))

    stations = [
        pltpu.make_async_copy(src, dst, in_sem.at[k])
        for k, (src, dst) in enumerate(((stx_ref, stx_buf), (sty_ref, sty_buf), (stz_ref, stz_buf)))
    ]
    spots = [
        pltpu.make_async_copy(src, dst, in_sem.at[3 + k])
        for k, (src, dst) in enumerate(((sx_ref, sx_buf), (sy_ref, sy_buf), (sz_ref, sz_buf)))
    ]
    seen_copy = pltpu.make_async_copy(obs_ref, seen_buf, in_sem.at[6])
    for load in stations:
        load.start()

    @pl.when(owner)
    def _():
        for load in spots:
            load.start()
        seen_copy.start()

    def piece(q, part):
        return full_ref.at[pl.ds(q * depth + part * half_depth, half_depth)]

    def copy(kind, q, brick, own=False):
        src = slow_ref.at[pl.ds(h * half_depth, half_depth)] if own else piece(q, h)
        return remote(src, piece(q, h), brick_send.at[kind, q], brick_recv.at[q], core, brick)

    def twin_copy(q):
        return remote(piece(q, h), piece(q, h), brick_send.at[2, q], twin_sem.at[q], twin, me)

    def along(k, up):
        dst = piece(me, h)
        src = slow_ref.at[pl.ds(h * half_depth, half_depth)]
        brick = me + LOW * k if up else me - LOW * k
        return remote(src, dst, line_sem.at[int(up), k], brick_recv.at[me], core, brick)

    def own_line(k, wait):
        def go(up):
            c = along(k, up)
            c.wait_send() if wait else c.start()

        pl.when(line >= k)(lambda: go(False))
        pl.when(line + k < lines)(lambda: go(True))

    def sends(q, own, wait):
        for kind, brick in ((0, first), (1, second)):
            c = copy(kind, q, brick, own)
            c.wait_send() if wait else c.start()

    own_copy = pltpu.make_async_copy(slow_ref, full_ref.at[pl.ds(me * depth, depth)], own_sem)
    seen_send = remote(obs_ref, seen_buf, word_send.at[0], word_recv.at[0], twin, me)
    spot_send = remote(spot_ref, spot_ref, word_send.at[1], word_recv.at[1], twin, me)

    near = jnp.minimum(line, reach) + jnp.minimum(lines - 1 - line, reach)
    pl.semaphore_wait(barrier, near + peers - 1)
    pl.when(owner)(seen_send.start)
    for k in range(1, reach + 1):
        own_line(k, False)
        if k == 1:
            sends(me, True, False)
    own_copy.start()

    def arrived(q):
        remote(piece(q, h), piece(q, h), brick_send.at[0, q], brick_recv.at[q], core, first).wait_recv()

    def on_line(base, i, act):
        pl.when((i <= reach) & (line >= i))(lambda: act(base - LOW * i, -1))
        pl.when((i <= reach) & (line + i < lines))(lambda: act(base + LOW * i, 1))

    def both(base, i, act):
        pl.when(i == 0)(lambda: act(base, 0))
        pl.when(i > 0)(lambda: on_line(base, i, act))

    def is_far(i):
        return (i == reach) & early

    def from_line(wait, i):
        def act(q, side):
            if not wait:
                arrived(q)
            sends(q, False, wait)

            @pl.when(is_far(i))
            def _():
                c = copy(3, q, corner)
                c.wait_send() if wait else c.start()

            c = twin_copy(q)
            c.wait_send() if wait else c.start()

        return act

    def from_first(wait, i):
        def act(q, side):
            if not wait:
                arrived(q)

            @pl.when(jnp.logical_not(is_far(i)))
            def _():
                c = copy(1, q, second)
                c.wait_send() if wait else c.start()

            c = twin_copy(q)
            c.wait_send() if wait else c.start()

        return act

    def from_second(wait):
        def act(q, side):
            if not wait:
                arrived(q)
            c = twin_copy(q)
            c.wait_send() if wait else c.start()

        return act

    def turn(i, wait):
        on_line(me, i, from_line(wait, i))
        both(first, i - 1, from_first(wait, i - 1))
        both(second, i - 1, from_second(wait))
        pl.when(i >= 2)(lambda: both(corner, i - 2, from_second(wait)))

    @pl.when(owner)
    def _():
        for load in spots:
            load.wait()
        sub = lax.broadcasted_iota(jnp.int32, spot_ref.shape, 0)
        spot_ref[...] = jnp.where(
            sub == 0, sx_buf[local], jnp.where(sub == 1, sy_buf[local], sz_buf[local])
        )

    for load in stations:
        load.wait()
    sty = sty_buf[...]
    stz = stz_buf[...]
    stx = stx_buf[...]
    away = stx - centre
    away = jnp.where(away < 0, away + grid_x, away)
    beyond = away < ring
    step_x = jnp.where(beyond, away, grid_x - 1 - away)
    row = (step_x * rows + (sty & (rows - 1))) * 8 + (sty >> shift)
    column = jnp.where(beyond, cells_z - 1 - (stz >> 1), stz >> 1)
    column = jnp.where(((stx + sty + stz) & 1) == h, column, -1)
    code_ref[0] = row
    code_ref[1] = column
    load_code = pltpu.make_async_copy(code_ref.at[0], code, code_sem)
    load_code.start()
    rec = row.shape[1]
    hit = lax.broadcasted_iota(jnp.int32, (cells_z, rec), 0) == column

    pl.when(owner)(seen_copy.wait)
    pl.when(owner)(spot_send.start)
    pl.when(jnp.logical_not(owner))(seen_send.wait_recv)
    seen = seen_buf[pl.ds(local, 1), :] * (1.0 / spacing)
    hi = seen.astype(jnp.bfloat16).astype(jnp.float32)
    rest = seen - hi
    mid = rest.astype(jnp.bfloat16).astype(jnp.float32)
    lo = rest - mid
    for n, value in enumerate((jnp.ones_like(seen), hi, mid, lo)):
        table[pl.ds(n * cells_z, cells_z), :] = jnp.where(hit, value, 0.0).astype(jnp.bfloat16)

    tiles = TALLY // 8
    blocks = tally_ref.shape[1] // tiles

    def tally(step):
        rows_of = lax.broadcasted_iota(jnp.int32, (TALLY, rec), 0) + step * TALLY
        pick = jnp.where(rows_of == row, 1.0, 0.0).astype(jnp.bfloat16)
        got = lax.dot_general(
            pick, table[...], (((1,), (1,)), ((), ())), preferred_element_type=jnp.float32
        )
        spot = pl.ds(step * tiles, tiles)
        tally_ref[0, spot] = got[:, :cells_z].reshape(tiles, 8, cells_z)
        total = got[:, cells_z : 2 * cells_z] + (
            got[:, 2 * cells_z : 3 * cells_z] + got[:, 3 * cells_z :]
        )
        tally_ref[1, spot] = total.reshape(tiles, 8, cells_z)

    tally_send = remote(
        tally_ref.at[pl.ds(0, 2)], tally_ref.at[pl.ds(2, 2)], word_send.at[2], word_recv.at[2], twin, me
    )

    def twins(low, high):
        @pl.loop(0, bricks)
        def _(q):
            gap = jnp.maximum(q // LOW - line, line - q // LOW)

            @pl.when((q != me) & (gap >= low) & (gap <= high))
            def _():
                remote(
                    piece(q, 1 - h), piece(q, 1 - h), brick_send.at[2, q], twin_sem.at[q], twin, me
                ).wait_recv()

    turns = reach if early else reach + 2

    @pl.loop(0, max(turns, blocks))
    def _(step):
        pl.when(step < turns)(lambda: turn(step + 1, False))
        pl.when(step < blocks)(lambda: tally(step))

    if early:
        for gap in range(reach + 1, lines):
            for away_line in (line - gap, line + gap):

                @pl.when((away_line >= 0) & (away_line < lines))
                def _():
                    @pl.loop(0, block)
                    def _(x):
                        full_ref[away_line * block + x] = jnp.ones((cells_y, cells_z), jnp.float32)

        both(corner, reach - 1, from_second(False))
    tally_send.start()
    own_copy.wait()
    twins(0, reach - 1 if early else reach)

    share = got_ref.shape[-1]
    quarter = picked.shape[0]
    pl.when(jnp.logical_not(owner))(spot_send.wait_recv)
    keep = slots_ref.shape[2]
    for t in range(depth):
        own_ref[t] = full_ref[me * depth + t, pl.ds(pl.multiple_of(core * keep, 8), keep), :]

    picks = ((line > 0) & (line < lines - 1)) if early else line >= 0

    def pick_line(n):
        if not early:
            return line
        return (line - 1) * 2 + n

    lane = lax.broadcasted_iota(jnp.int32, (8, cells_z), 1)
    sub = lax.broadcasted_iota(jnp.int32, (8, cells_z), 0)
    sub_first = sub == 0
    sub_last = sub == 7
    upper = lane >= half_z
    inner = jnp.where(upper, cells_z - 1 - lane, lane)
    parity = [lax.rem(q + h, 2) for q in range(2)]
    cell_z = [inner * 2 + jnp.where(upper, 1 - p, p) for p in parity]
    from_low = [(lane & 1) == p for p in parity]
    edge_z = [(lane & (half_z - 1)) == p * (half_z - 1) for p in parity]
    slide = [1 + p * (cells_z - 2) for p in parity]
    mirror = cells_z - 1 - lane

    def slot(i, v):
        return (i + 1) * rows + v

    sx = spot_ref[0:1, :]
    sy = spot_ref[1:2, :]
    sz = spot_ref[2:3, :]
    unit = (start_slowness * spacing) ** 2
    flat = []
    for q in range(2):
        dz = (cell_z[q] - sz).astype(jnp.float32)
        dz = dz * dz
        for v in range(rows):
            dy = (sub * rows + v - sy).astype(jnp.float32)
            flat.append((dy * dy + dz) * unit)

    def prepare(quad):
        for j in range(4):
            i = quad * 4 + j
            x_low = centre - 1 - i
            x_low = jnp.where(x_low < 0, x_low + grid_x, x_low)
            x_high = centre + i
            x_high = jnp.where(x_high >= grid_x, x_high - grid_x, x_high)
            dx = (jnp.where(upper, x_high, x_low) - sx).astype(jnp.float32)
            dx = dx * dx * unit
            for v in range(rows):
                q = (j + 1 + v) % 2
                low = full_ref[x_low, pl.ds(v, 8, stride=rows), :]
                high = full_ref[x_high, pl.ds(v, 8, stride=rows), :]
                pair_of = (
                    (chain, chain_cost, q, jnp.where(from_low[q], low, high)),
                    (other, other_cost, 1 - q, jnp.where(from_low[q], high, low)),
                )
                for field, cost, k, natural in pair_of if q else pair_of[::-1]:
                    slow = jnp.take_along_axis(natural, cell_z[k], axis=1)
                    square = dx + flat[k * rows + v]
                    start = square * lax.rsqrt(jnp.maximum(square, unit * 0.5))
                    cost[i * rows + v] = (2.0 * half_step) * slow
                    field[slot(i, v)] = start + half_step * slow

    @pl.loop(0, (span if early else ring) // 4)
    def _(quad):
        prepare(quad)

    cuts = {
        b: jnp.where(upper, grid_x - centre, centre) == b for b in range(half, ring, half) if (b // half) % 2
    }

    def swing(one):
        return jnp.take_along_axis(one, mirror, axis=1)

    def across_z(one, k):
        return pltpu.roll(one, slide[k], 1)

    def y_up(cur, v):
        return cur[v + 1] if v + 1 < rows else pltpu.roll(cur[0], 7, 0)

    def y_down(cur, v):
        return cur[v - 1] if v else pltpu.roll(cur[rows - 1], 1, 0)

    def layer_of(ref, i):
        return [ref[slot(i, v)] for v in range(rows)]

    def sweep(dst, cost, src, turned, low_end, high_end):
        cur = layer_of(src, low_end)
        prev = layer_of(src, low_end - 1) if low_end else [swing(one) for one in cur]
        for i in range(low_end, high_end):
            after_of = layer_of(src, i + 1) if i + 1 < ring else [swing(one) for one in cur]
            for v in range(rows):
                q = (i + 1 + v) % 2
                before = prev[v]
                after = after_of[v]
                if i in cuts:
                    before = jnp.where(cuts[i], big_value, before)
                if i + 1 in cuts:
                    after = jnp.where(cuts[i + 1], big_value, after)
                up = y_up(cur, v)
                down = y_down(cur, v)
                if v + 1 == rows:
                    up = jnp.where(sub_last, big_value, up)
                if v == 0:
                    down = jnp.where(sub_first, big_value, down)
                k = q ^ turned
                across = jnp.where(edge_z[k], cur[v], across_z(cur[v], k))
                low = jnp.minimum(across, cur[v])
                for value in (before, after, down, up):
                    low = jnp.minimum(low, value)
                dst[slot(i, v)] = jnp.minimum(dst[slot(i, v)], low + cost[i * rows + v])
            prev, cur = cur, after_of

    assert ITERS % 2 == 0

    def step_of(j, low_end, high_end):
        if j % 2:
            sweep(other, other_cost, chain, 1, low_end, high_end)
        else:
            sweep(chain, chain_cost, other, 0, low_end, high_end)

    if early:
        for j in range(1, ITERS + 1):
            step_of(j, 0, span - j)
            if j == ITERS // 2:
                both(first, reach, from_first(False, reach))
                both(second, reach, from_second(False))
        both(corner, reach, from_second(False))
        twins(reach, reach)

        @pl.loop(span // 4, ring // 4)
        def _(quad):
            prepare(quad)

        for j in range(1, ITERS + 1):
            step_of(j, span - j, ring)
    else:

        @pl.loop(0, ITERS // 2)
        def _(_step):
            step_of(1, 0, ring)
            step_of(2, 0, ring)

    @pl.loop(0, ring)
    def _(i):
        for v in range(rows):
            chain[slot(i, v)] = (chain[slot(i, v)] - 0.5 * chain_cost[i * rows + v]) * (1.0 / spacing)

    for v in range(rows):
        chain[slot(-1, v)] = swing(chain[slot(0, v)])

    stops = [0] + [(2 + n * half) * rows for n in range(1, span // half + 1)]
    time_copies = []
    for n, (low, high) in enumerate(zip(stops, stops[1:])):
        part_of = pl.ds(low, high - low)
        time_copies.append(
            remote(chain.at[part_of], twin_time.at[part_of], time_send.at[n], time_recv.at[n], twin, me)
        )
    for copy_of in time_copies:
        copy_of.start()

    load_code.wait()
    unroll = 16

    def pick(n):
        whose = pick_line(n)
        place_of = pl.multiple_of(whose * quarter, 128)

        @pl.loop(0, quarter // unroll)
        def _(m):
            for j in range(unroll):
                r = m * unroll + j
                at = code[0, place_of + r]
                picked[pl.ds(r, 1), :] = chain[(at >> 3) + rows, pl.ds(at & 7, 1), :]

        column = code_ref[1, :, pl.ds(place_of, quarter)]
        turned = jnp.transpose(picked[...])
        here = lax.broadcasted_iota(jnp.int32, turned.shape, 0) == column
        arrived_at = jnp.sum(jnp.where(here, turned, 0.0), axis=0, keepdims=True) * spacing
        for k in range(LOW):
            part[n * LOW + k] = arrived_at[:, k * share : (k + 1) * share]

    pl.when(picks)(lambda: pick(0))

    for v in range(rows):
        chain_field[slot(span - 2, v)] = jnp.zeros((8, cells_z), jnp.float32)
        chain_field[slot(span - 1, v)] = jnp.zeros((8, cells_z), jnp.float32)
        chain_field[slot(span, v)] = jnp.zeros((8, cells_z), jnp.float32)
        other_field[slot(span, v)] = jnp.zeros((8, cells_z), jnp.float32)

    bound = jnp.where(upper, grid_x - centre, centre)
    tally_send.wait_recv()

    def weigh(at, i, own, theirs, weight, supply, field, tally, turned):
        cur = [theirs[slot(at, v)] for v in range(rows)]
        cut_before = bound == at
        cut_after = bound == at + 1
        for v in range(rows):
            q = (i + 1 + v) % 2
            one = own[slot(at, v)]

            def gain(value):
                return jnp.maximum(value - one, 0.0)

            before = gain(theirs[slot(at - 1, v)])
            after = gain(theirs[slot(at + 1, v)])
            if i % half == 0:
                before = jnp.where(cut_before, 0.0, before)
            if (i + 1) % half == 0:
                after = jnp.where(cut_after, 0.0, after)
            up = gain(y_up(cur, v))
            down = gain(y_down(cur, v))
            if v + 1 == rows:
                up = jnp.where(sub_last, 0.0, up)
            if v == 0:
                down = jnp.where(sub_first, 0.0, down)
            k = q ^ turned
            across = jnp.where(edge_z[k], 0.0, gain(across_z(cur[v], k)))
            parts = (before, after, down, up, gain(cur[v]), across)
            total = ((parts[0] + parts[1]) + (parts[2] + parts[3])) + (parts[4] + parts[5])
            inverse = 1.0 / (1.0 + total)
            spot = at * rows + v
            for n, gained in enumerate(parts):
                weight[n, spot] = gained * inverse
            value = (tally_ref[tally, spot] * one - tally_ref[tally + 1, spot]) * inverse
            supply[spot] = value
            if turned:
                field[slot(at, v)] = value

    @pl.loop(0, span // half)
    def _(chunk):
        for n, copy_of in enumerate(time_copies):
            pl.when(chunk == n)(copy_of.wait_recv)
        for i in range(half):
            at = chunk * half + i
            weigh(at, i, twin_time, chain, other_weight, other_supply, other_field, 2, 1)
            weigh(at, i, chain, twin_time, chain_weight, chain_supply, chain_field, 0, 0)

    for v in range(rows):
        other_field[slot(-1, v)] = swing(other_field[slot(0, v)])

    def backward(count, dst, weight, supply, src, turned):
        cur = layer_of(src, 0)
        prev = [swing(one) for one in cur]
        for i in range(count):
            after_of = layer_of(src, i + 1)
            for v in range(rows):
                q = (i + 1 + v) % 2
                spot = i * rows + v
                acc = supply[spot] + weight[0, spot] * prev[v]
                acc = acc + weight[1, spot] * after_of[v]
                side = weight[2, spot] * y_down(cur, v) + weight[3, spot] * y_up(cur, v)
                across = across_z(cur[v], q ^ turned)
                acc = (acc + side) + (weight[4, spot] * cur[v] + weight[5, spot] * across)
                dst[slot(i, v)] = acc
            prev, cur = cur, after_of

    def rounds(first, times):
        count = half + ITERS - first

        @pl.loop(0, times)
        def _(_step):
            backward(count, chain_field, chain_weight, chain_supply, other_field, 0)
            backward(count - 1, other_field, other_weight, other_supply, chain_field, 1)

    rounds(2, 3)
    rounds(8, 2)
    rounds(12, 2)
    backward(half, chain_field, chain_weight, chain_supply, other_field, 0)

    for k in range(LOW):
        for t in range(0, depth, 2):
            low_side = k < LOW // 2
            near, next_to = (
                (half - 1 - (k * depth + t + n)) if low_side else (k * depth + t + n - half) for n in range(2)
            )
            for v in range(rows):
                a = chain_field[slot(near, v)]
                b = chain_field[slot(next_to, v)]
                merged = jnp.where(upper, swing(b), a) if low_side else jnp.where(upper, b, swing(a))
                packed[k, t // 2, pl.ds(v, 8, stride=rows), :] = merged

    keep = slots_ref.shape[2]

    def ship(k):
        c, b, p = peer(k)
        return remote(
            packed.at[p, :, pl.ds(c * keep, keep)], slots_ref.at[mine], send_sem.at[k], recv_sem.at[mine], c, b
        )

    for k in range(1, peers):
        ship(k).start()
    stay = pltpu.make_async_copy(
        packed.at[place, :, pl.ds(core * keep, keep)], slots_ref.at[mine], self_sem
    )
    stay.start()

    target = core - h + place // 2

    def word(n, k):
        return remote(
            part.at[n * LOW + k],
            got_ref.at[local, h],
            part_send.at[n * LOW + k],
            part_recv.at[local, h],
            target,
            pick_line(n) * LOW + k,
        )

    def home(n, k):
        return (target == core) & (pick_line(n) * LOW + k == me)

    def post(n):
        for k in range(LOW):
            pl.when(jnp.logical_not(home(n, k)))(word(n, k).start)

            @pl.when(home(n, k))
            def _():
                got_ref[local, h] = part[n * LOW + k]

    def posted(n):
        for k in range(LOW):
            pl.when(jnp.logical_not(home(n, k)))(word(n, k).wait_send)

    pl.when(picks)(lambda: post(0))
    if early:
        pl.when(picks)(lambda: pick(1))
        pl.when(picks)(lambda: post(1))

    def word_in(n, side):
        return remote(
            part.at[0], got_ref.at[n, side], part_send.at[0], part_recv.at[n, side], core, me
        )

    for n in range(2):
        for side in range(2):
            from_me = picks & (place == 2 * h + n) & (h == side)
            pl.when(jnp.logical_not(from_me))(word_in(n, side).wait_recv)
    for k in range(1, peers):
        m = lax.rem(mine + k, peers)
        remote(
            packed.at[0, :, pl.ds(0, keep)], slots_ref.at[m], send_sem.at[k], recv_sem.at[m], core, me
        ).wait_recv()
    for k in range(1, peers):
        ship(k).wait_send()
    pl.when(picks)(lambda: posted(0))
    if early:
        pl.when(picks)(lambda: posted(1))
    stay.wait()
    for copy_of in time_copies:
        copy_of.wait_send()
    tally_send.wait_send()
    sends(me, True, True)
    for k in range(1, reach + 1):
        own_line(k, True)

    @pl.loop(1, reach + 3)
    def _(i):
        turn(i, True)

    @pl.when(owner)
    def _():
        seen_send.wait_send()
        spot_send.wait_send()


def finish_kernel(cores, slots_ref, got_ref, own_ref, out_ref, arr_ref):
    depth, keep, cells_z = out_ref.shape
    half_z = cells_z // 2
    lane = lax.broadcasted_iota(jnp.int32, (8, cells_z), 1)
    sub = lax.broadcasted_iota(jnp.int32, (8, cells_z), 0)
    upper = lane >= half_z
    plain = ((sub + jnp.where(upper, 1, 0)) & 1) == 0
    join = jnp.where((lane & 1) == 0, lane >> 1, cells_z - 1 - (lane >> 1))
    mirror = cells_z - 1 - lane
    for t in range(depth // 2):
        for y in range(0, keep, 8):
            sums = []
            for colour in range(2):
                total = None
                for c in range(colour, cores, 2):
                    for k in range(LOW):
                        one = slots_ref[c * LOW + k, t, pl.ds(y, 8), :]
                        total = one if total is None else total + one
                sums.append(total)
            even = jnp.where(plain, sums[0], sums[1])
            odd = jnp.where(plain, sums[1], sums[0])
            moved = jnp.take_along_axis(jnp.where(upper, even, odd), mirror, axis=1)
            for n, packed in enumerate((jnp.where(upper, moved, even), jnp.where(upper, odd, moved))):
                value = jnp.take_along_axis(packed, join, axis=1)
                slow = own_ref[2 * t + n, pl.ds(y, 8), :]
                out_ref[2 * t + n, pl.ds(y, 8), :] = (slow * spacing) * value
    for n in range(2):
        arr_ref[pl.ds(n, 1), :] = got_ref[n, 0] + got_ref[n, 1]


def per_device(slowness, source_x, source_y, source_z, station_x, station_y, station_z, observed):
    bricks = lax.axis_size("brick")
    cores = lax.axis_size("src")
    depth, cells_y, cells_z = slowness.shape
    grid_x = depth * bricks
    rec = station_x.shape[0]
    rows = cells_y // 8
    ring = grid_x // 2
    half = LOW * depth // 2
    span = half + ITERS
    assert source_x.shape[0] == 2 and bricks % LOW == 0 and cores % 2 == 0
    assert half % 2 == 0 and span % half == 0 and span + 1 <= ring and (span * rows * 8) % TALLY == 0
    assert span % 4 == 0 and ring % 4 == 0
    f32 = jnp.float32
    i32 = jnp.int32
    share = rec // bricks
    quarter = share * LOW
    keep = cells_y // cores
    ring_shape = ((ring + 2) * rows, 8, cells_z)
    span_shape = ((span + 2) * rows, 8, cells_z)
    dma = pltpu.SemaphoreType.DMA
    slots, got, own = pl.pallas_call(
        functools.partial(solve_kernel, bricks, cores),
        name="solve",
        out_shape=(
            jax.ShapeDtypeStruct((LOW * cores, depth // 2, keep, cells_z), f32),
            jax.ShapeDtypeStruct((2, 2, 1, share), f32),
            jax.ShapeDtypeStruct((depth, keep, cells_z), f32),
        ),
        in_specs=[HBM] * 8,
        out_specs=(VMEM, VMEM, VMEM),
        scratch_shapes=[
            pltpu.VMEM((grid_x, cells_y, cells_z), f32),
            pltpu.VMEM((4, span * rows, 8, cells_z), f32),
            pltpu.VMEM((2, 1, rec), i32),
            pltpu.VMEM((8, cells_z), i32),
            pltpu.VMEM((4 * cells_z, rec), jnp.bfloat16),
            pltpu.VMEM(ring_shape, f32),
            pltpu.VMEM(ring_shape, f32),
            pltpu.VMEM((ring * rows, 8, cells_z), f32),
            pltpu.VMEM((ring * rows, 8, cells_z), f32),
            pltpu.VMEM(span_shape, f32),
            pltpu.VMEM((6, span * rows, 8, cells_z), f32),
            pltpu.VMEM((6, span * rows, 8, cells_z), f32),
            pltpu.VMEM((span * rows, 8, cells_z), f32),
            pltpu.VMEM((span * rows, 8, cells_z), f32),
            pltpu.VMEM(span_shape, f32),
            pltpu.VMEM(span_shape, f32),
            pltpu.VMEM((LOW, depth // 2, cells_y, cells_z), f32),
            pltpu.VMEM((quarter, cells_z), f32),
            pltpu.VMEM((2 * LOW, 1, share), f32),
            pltpu.VMEM((1, rec), i32),
            pltpu.VMEM((1, rec), i32),
            pltpu.VMEM((1, rec), i32),
            pltpu.VMEM(observed.shape, f32),
            pltpu.SMEM((1, rec), i32),
            pltpu.SMEM((2,), i32),
            pltpu.SMEM((2,), i32),
            pltpu.SMEM((2,), i32),
            dma((2, bricks // LOW)),
            dma((4, bricks)),
            dma((bricks,)),
            dma((bricks,)),
            dma,
            dma((7,)),
            dma((3,)),
            dma((3,)),
            dma,
            dma((span // half,)),
            dma((span // half,)),
            dma((LOW * cores,)),
            dma((LOW * cores,)),
            dma((2 * LOW,)),
            dma((2, 2)),
            dma,
        ],
        compiler_params=pltpu.CompilerParams(
            collective_id=0, has_side_effects=True, vmem_limit_bytes=SOLVE_VMEM
        ),
    )(
        *(
            pltpu.with_memory_space_constraint(a, pltpu.HBM)
            for a in (
                slowness,
                source_x,
                source_y,
                source_z,
                station_x[None],
                station_y[None],
                station_z[None],
                observed,
            )
        )
    )

    return tuple(
        pl.pallas_call(
            functools.partial(finish_kernel, cores),
            name="finish",
            out_shape=(
                jax.ShapeDtypeStruct((depth, keep, cells_z), f32),
                jax.ShapeDtypeStruct((2, share), f32),
            ),
            in_specs=[VMEM] * 3,
            compiler_params=pltpu.CompilerParams(vmem_limit_bytes=FINISH_VMEM),
        )(slots, got, own)
    )


def solution(mesh):
    in_specs = (P("brick", None, None), P("src"), P("src"), P("src"), P(), P(), P(), P("src", None))
    out_specs = (P("brick", "src", None), P("src", "brick"))
    return jax.shard_map(
        per_device, mesh=mesh, in_specs=in_specs, out_specs=out_specs, check_vma=False
    )
```

time: 45.4 us -> 41.1 us (0.905)
  Pallas kernels: 44.6 us -> 39.9 us
    pallas_call x2 -> x1, Pallas kernels: 43.8 us -> 39.1 us  [per_device(): pl.pallas_call(functools.partial(solve_kernel, bricks, cores), name='solv...]
where the time goes in v4:
time: 41.1 us; the launch traced here: 40.6 us
  Pallas kernels  39.9 us (97%)
  between operations  0.64 us (2%)
    pallas_call x1, Pallas kernels, per_device(): pl.pallas_call(functools.partial(solve_kernel, bricks, cores), name='solv...  39.1 us

profile of v4, /device:TPU:0, one launch (start us, length us, event | category | flops | bytes accessed | tf_op | source)
XLA Modules:
  0.0 40.6 jit_solution(8101498448234534354)
XLA Ops:
  0.6 39.1 %solve.1 = (f32[8,2,32,128]{3,2,1,0:T(8,128)S(1)}, f32[2,2,1,128]{3,2,1,0:T(1,128)S(1)}, f32[4,32,128]{2,1,0:T(8,128)S(1)}) custom-call(f32[4,64,128]{2,1,0:T(8,128)} %slow_ref.1, s32[2]{0:T(128)} %sx_ref.1, s32[2]{0:T(128)} %sy_ref.1, s32[2]{0:T(128)} %sz_ref.1, s32[1,2048]{1,0:T(1,128)} %bitcast.3, s32[1,2048]{1,0:T(1,128)} %bitcast.4, s32[1,2048]{1,0:T(1,128)} %bitcast.5, ...), custom_call_target="tpu_custom_call" | custom-call | tf_op jit(solution)/shard_map/solve/pallas_call | solution.py:778
  39.8 0.8 %finish.1 = (f32[4,32,128]{2,1,0:T(8,128)}, f32[2,128]{1,0:T(2,128)}) custom-call(f32[8,2,32,128]{3,2,1,0:T(8,128)S(1)} %get-tuple-element.5.slots_ref, f32[2,2,1,128]{3,2,1,0:T(1,128)S(1)} %get-tuple-element.6.got_ref, f32[4,32,128]{2,1,0:T(8,128)S(1)} %get-tuple-element.7.own_ref), custom_call_target="tpu_custom_call" | custom-call | tf_op jit(solution)/shard_map/finish/pallas_call | solution.py:853

commit v5 on v4

--- a/solution.py
+++ b/solution.py
@@ -161,33 +161,39 @@
             load.start()
         seen_copy.start()
 
-    def piece(q, part):
-        return full_ref.at[pl.ds(q * depth + part * half_depth, half_depth)]
-
-    def copy(kind, q, brick, own=False):
-        src = slow_ref.at[pl.ds(h * half_depth, half_depth)] if own else piece(q, h)
-        return remote(src, piece(q, h), brick_send.at[kind, q], brick_recv.at[q], core, brick)
-
-    def twin_copy(q):
-        return remote(piece(q, h), piece(q, h), brick_send.at[2, q], twin_sem.at[q], twin, me)
-
-    def along(k, up):
-        dst = piece(me, h)
-        src = slow_ref.at[pl.ds(h * half_depth, half_depth)]
+    subs = brick_recv.shape[1]
+    unit_depth = half_depth // subs
+
+    def piece(q, part_of, u):
+        return full_ref.at[pl.ds(q * depth + part_of * half_depth + u * unit_depth, unit_depth)]
+
+    def mine_of(u):
+        return slow_ref.at[pl.ds(h * half_depth + u * unit_depth, unit_depth)]
+
+    def copy(kind, q, u, brick, own=False):
+        src = mine_of(u) if own else piece(q, h, u)
+        return remote(src, piece(q, h, u), brick_send.at[kind, q, u], brick_recv.at[q, u], core, brick)
+
+    def twin_copy(q, u):
+        return remote(piece(q, h, u), piece(q, h, u), brick_send.at[2, q, u], twin_sem.at[q, u], twin, me)
+
+    def along(k, u, up):
         brick = me + LOW * k if up else me - LOW * k
-        return remote(src, dst, line_sem.at[int(up), k], brick_recv.at[me], core, brick)
-
-    def own_line(k, wait):
+        return remote(
+            mine_of(u), piece(me, h, u), line_sem.at[int(up), k, u], brick_recv.at[me, u], core, brick
+        )
+
+    def own_line(k, u, wait):
         def go(up):
-            c = along(k, up)
+            c = along(k, u, up)
             c.wait_send() if wait else c.start()
 
         pl.when(line >= k)(lambda: go(False))
         pl.when(line + k < lines)(lambda: go(True))
 
-    def sends(q, own, wait):
+    def sends(q, u, own, wait):
         for kind, brick in ((0, first), (1, second)):
-            c = copy(kind, q, brick, own)
+            c = copy(kind, q, u, brick, own)
             c.wait_send() if wait else c.start()
 
     own_copy = pltpu.make_async_copy(slow_ref, full_ref.at[pl.ds(me * depth, depth)], own_sem)
@@ -197,71 +203,90 @@
     near = jnp.minimum(line, reach) + jnp.minimum(lines - 1 - line, reach)
     pl.semaphore_wait(barrier, near + peers - 1)
     pl.when(owner)(seen_send.start)
-    for k in range(1, reach + 1):
-        own_line(k, False)
-        if k == 1:
-            sends(me, True, False)
+    for u in range(subs):
+        own_line(1, u, False)
+        sends(me, u, True, False)
+        if early:
+            copy(3, me, u, corner, True).start()
+    for k in range(2, reach + 1):
+        for u in range(subs):
+            own_line(k, u, False)
     own_copy.start()
 
-    def arrived(q):
-        remote(piece(q, h), piece(q, h), brick_send.at[0, q], brick_recv.at[q], core, first).wait_recv()
-
-    def on_line(base, i, act):
-        pl.when((i <= reach) & (line >= i))(lambda: act(base - LOW * i, -1))
-        pl.when((i <= reach) & (line + i < lines))(lambda: act(base + LOW * i, 1))
-
-    def both(base, i, act):
-        pl.when(i == 0)(lambda: act(base, 0))
-        pl.when(i > 0)(lambda: on_line(base, i, act))
+    def arrived(q, u):
+        remote(
+            piece(q, h, u), piece(q, h, u), brick_send.at[0, q, u], brick_recv.at[q, u], core, first
+        ).wait_recv()
+
+    def on_line(base_of, i, act):
+        pl.when((i <= reach) & (line >= i))(lambda: act(base_of - LOW * i))
+        pl.when((i <= reach) & (line + i < lines))(lambda: act(base_of + LOW * i))
+
+    def both(base_of, i, act):
+        pl.when(i == 0)(lambda: act(base_of))
+        pl.when(i > 0)(lambda: on_line(base_of, i, act))
 
     def is_far(i):
-        return (i == reach) & early
-
-    def from_line(wait, i):
-        def act(q, side):
+        return ((i == reach) | (i == 0)) & early
+
+    def from_line(wait, i, u):
+        def act(q):
             if not wait:
-                arrived(q)
-            sends(q, False, wait)
+                arrived(q, u)
+            sends(q, u, False, wait)
 
             @pl.when(is_far(i))
             def _():
-                c = copy(3, q, corner)
+                c = copy(3, q, u, corner)
                 c.wait_send() if wait else c.start()
 
-            c = twin_copy(q)
+            c = twin_copy(q, u)
             c.wait_send() if wait else c.start()
 
         return act
 
-    def from_first(wait, i):
-        def act(q, side):
+    def from_first(wait, i, u):
+        def act(q):
             if not wait:
-                arrived(q)
+                arrived(q, u)
 
             @pl.when(jnp.logical_not(is_far(i)))
             def _():
-                c = copy(1, q, second)
+                c = copy(1, q, u, second)
                 c.wait_send() if wait else c.start()
 
-            c = twin_copy(q)
+            c = twin_copy(q, u)
             c.wait_send() if wait else c.start()
 
         return act
 
-    def from_second(wait):
-        def act(q, side):
+    def from_second(wait, u):
+        def act(q):
             if not wait:
-                arrived(q)
-            c = twin_copy(q)
+                arrived(q, u)
+            c = twin_copy(q, u)
             c.wait_send() if wait else c.start()
 
         return act
 
-    def turn(i, wait):
-        on_line(me, i, from_line(wait, i))
-        both(first, i - 1, from_first(wait, i - 1))
-        both(second, i - 1, from_second(wait))
-        pl.when(i >= 2)(lambda: both(corner, i - 2, from_second(wait)))
+    def line_turn(i, wait):
+        @pl.loop(0, subs)
+        def _(u):
+            on_line(me, i, from_line(wait, i, u))
+
+    def side_turn(i, wait, with_line=False):
+        @pl.loop(0, subs)
+        def _(u):
+            if with_line:
+                on_line(me, i, from_line(wait, i, u))
+            both(first, i - 1, from_first(wait, i - 1, u))
+            both(second, i - 1, from_second(wait, u))
+            pl.when(i >= 2)(lambda: both(corner, i - 2, from_second(wait, u)))
+
+    def corner_turn(i):
+        @pl.loop(0, subs)
+        def _(u):
+            both(corner, i, from_second(False, u))
 
     @pl.when(owner)
     def _():
@@ -322,25 +347,34 @@
         tally_ref.at[pl.ds(0, 2)], tally_ref.at[pl.ds(2, 2)], word_send.at[2], word_recv.at[2], twin, me
     )
 
+    def twin_in(q):
+        for u in range(subs):
+            remote(
+                piece(q, 1 - h, u), piece(q, 1 - h, u), brick_send.at[2, q, u], twin_sem.at[q, u], twin, me
+            ).wait_recv()
+
     def twins(low, high):
-        @pl.loop(0, bricks)
-        def _(q):
-            gap = jnp.maximum(q // LOW - line, line - q // LOW)
-
-            @pl.when((q != me) & (gap >= low) & (gap <= high))
+        for i in range(low, high + 1):
+            for base_of in (me, first, second, corner):
+                if i:
+                    on_line(base_of, i, twin_in)
+                elif base_of is not me:
+                    twin_in(base_of)
+
+    if early:
+
+        @pl.loop(0, blocks)
+        def _(step):
+            tally(step)
+
+            @pl.when(step == 0)
             def _():
-                remote(
-                    piece(q, 1 - h), piece(q, 1 - h), brick_send.at[2, q], twin_sem.at[q], twin, me
-                ).wait_recv()
-
-    turns = reach if early else reach + 2
-
-    @pl.loop(0, max(turns, blocks))
-    def _(step):
-        pl.when(step < turns)(lambda: turn(step + 1, False))
-        pl.when(step < blocks)(lambda: tally(step))
-
-    if early:
+                line_turn(1, False)
+                side_turn(1, False)
+
+        side_turn(reach, False)
+        line_turn(reach, False)
+
         for gap in range(reach + 1, lines):
             for away_line in (line - gap, line + gap):
 
@@ -350,10 +384,16 @@
                     def _(x):
                         full_ref[away_line * block + x] = jnp.ones((cells_y, cells_z), jnp.float32)
 
-        both(corner, reach - 1, from_second(False))
+    else:
+
+        @pl.loop(0, max(reach + 2, blocks))
+        def _(step):
+            pl.when(step < reach + 2)(lambda: side_turn(step + 1, False, True))
+            pl.when(step < blocks)(lambda: tally(step))
+
+    own_copy.wait()
     tally_send.start()
-    own_copy.wait()
-    twins(0, reach - 1 if early else reach)
+    twins(0, 0 if early else reach)
 
     share = got_ref.shape[-1]
     quarter = picked.shape[0]
@@ -421,7 +461,7 @@
                     cost[i * rows + v] = (2.0 * half_step) * slow
                     field[slot(i, v)] = start + half_step * slow
 
-    @pl.loop(0, (span if early else ring) // 4)
+    @pl.loop(0, (half if early else ring) // 4)
     def _(quad):
         prepare(quad)
 
@@ -479,21 +519,62 @@
         else:
             sweep(chain, chain_cost, other, 0, low_end, high_end)
 
+    stops = [0, 1 + half, 1 + 2 * half, 1 + span]
+    time_copies = []
+    for n, (low, high) in enumerate(zip(stops, stops[1:])):
+        part_of = pl.ds(low * rows, (high - low) * rows)
+        time_copies.append(
+            remote(chain.at[part_of], twin_time.at[part_of], time_send.at[n], time_recv.at[n], twin, me)
+        )
+
+    def scale_times(low_end, high_end):
+        if low_end == 0:
+            for v in range(rows):
+                one = (chain[slot(0, v)] - 0.5 * chain_cost[v]) * (1.0 / spacing)
+                chain[slot(-1, v)] = swing(one)
+
+        @pl.loop(low_end, high_end)
+        def _(i):
+            for v in range(rows):
+                chain[slot(i, v)] = (chain[slot(i, v)] - 0.5 * chain_cost[i * rows + v]) * (1.0 / spacing)
+
     if early:
-        for j in range(1, ITERS + 1):
-            step_of(j, 0, span - j)
-            if j == ITERS // 2:
-                both(first, reach, from_first(False, reach))
-                both(second, reach, from_second(False))
-        both(corner, reach, from_second(False))
+        assert reach == 2 and span == 3 * half
+
+        def stage(done, ready, hook=None):
+            for j in range(1, ITERS + 1):
+                low_end = max(done - j, 0)
+                high_end = ready if ready == ring else ready - j
+                if high_end > low_end:
+                    step_of(j, low_end, high_end)
+                if hook is not None and j == ITERS // 2:
+                    hook()
+
+        stage(0, half)
+        corner_turn(reach - 1)
+        twins(1, reach - 1)
+
+        @pl.loop(half // 4, span // 4)
+        def _(quad):
+            prepare(quad)
+
+        def relay_far():
+            @pl.loop(0, subs)
+            def _(u):
+                both(first, reach, from_first(False, reach, u))
+                both(second, reach, from_second(False, u))
+
+        stage(half, span, relay_far)
+        scale_times(0, half)
+        corner_turn(reach)
+        time_copies[0].start()
         twins(reach, reach)
 
         @pl.loop(span // 4, ring // 4)
         def _(quad):
             prepare(quad)
 
-        for j in range(1, ITERS + 1):
-            step_of(j, span - j, ring)
+        stage(span, ring)
     else:
 
         @pl.loop(0, ITERS // 2)
@@ -501,46 +582,35 @@
             step_of(1, 0, ring)
             step_of(2, 0, ring)
 
-    @pl.loop(0, ring)
-    def _(i):
-        for v in range(rows):
-            chain[slot(i, v)] = (chain[slot(i, v)] - 0.5 * chain_cost[i * rows + v]) * (1.0 / spacing)
-
-    for v in range(rows):
-        chain[slot(-1, v)] = swing(chain[slot(0, v)])
-
-    stops = [0] + [(2 + n * half) * rows for n in range(1, span // half + 1)]
-    time_copies = []
-    for n, (low, high) in enumerate(zip(stops, stops[1:])):
-        part_of = pl.ds(low, high - low)
-        time_copies.append(
-            remote(chain.at[part_of], twin_time.at[part_of], time_send.at[n], time_recv.at[n], twin, me)
-        )
-    for copy_of in time_copies:
+    if not early:
+        scale_times(0, half)
+        time_copies[0].start()
+    scale_times(half, ring)
+    for copy_of in time_copies[1:]:
         copy_of.start()
 
     load_code.wait()
     unroll = 16
 
-    def pick(n):
-        whose = pick_line(n)
-        place_of = pl.multiple_of(whose * quarter, 128)
-
-        @pl.loop(0, quarter // unroll)
+    def pick_rows(n, low_end, high_end):
+        place_of = pl.multiple_of(pick_line(n) * quarter, 128)
+
+        @pl.loop(low_end // unroll, high_end // unroll)
         def _(m):
             for j in range(unroll):
                 r = m * unroll + j
                 at = code[0, place_of + r]
                 picked[pl.ds(r, 1), :] = chain[(at >> 3) + rows, pl.ds(at & 7, 1), :]
 
+    def pick(n, low_end):
+        pick_rows(n, low_end, quarter)
+        place_of = pl.multiple_of(pick_line(n) * quarter, 128)
         column = code_ref[1, :, pl.ds(place_of, quarter)]
         turned = jnp.transpose(picked[...])
         here = lax.broadcasted_iota(jnp.int32, turned.shape, 0) == column
         arrived_at = jnp.sum(jnp.where(here, turned, 0.0), axis=0, keepdims=True) * spacing
         for k in range(LOW):
             part[n * LOW + k] = arrived_at[:, k * share : (k + 1) * share]
-
-    pl.when(picks)(lambda: pick(0))
 
     for v in range(rows):
         chain_field[slot(span - 2, v)] = jnp.zeros((8, cells_z), jnp.float32)
@@ -587,14 +657,21 @@
             if turned:
                 field[slot(at, v)] = value
 
-    @pl.loop(0, span // half)
+    def weigh_both(at, i):
+        weigh(at, i, twin_time, chain, other_weight, other_supply, other_field, 2, 1)
+        weigh(at, i, chain, twin_time, chain_weight, chain_supply, chain_field, 0, 0)
+
+    time_copies[0].wait_recv()
+    for i in range(half - 1):
+        weigh_both(i, i)
+    pl.when(picks)(lambda: pick_rows(0, 0, quarter // 2))
+
+    @pl.loop(0, span // half - 1)
     def _(chunk):
-        for n, copy_of in enumerate(time_copies):
+        for n, copy_of in enumerate(time_copies[1:]):
             pl.when(chunk == n)(copy_of.wait_recv)
-        for i in range(half):
-            at = chunk * half + i
-            weigh(at, i, twin_time, chain, other_weight, other_supply, other_field, 2, 1)
-            weigh(at, i, chain, twin_time, chain_weight, chain_supply, chain_field, 0, 0)
+        for i in range(half - 1, 2 * half - 1):
+            weigh_both(chunk * half + i, i)
 
     for v in range(rows):
         other_field[slot(-1, v)] = swing(other_field[slot(0, v)])
@@ -615,8 +692,8 @@
                 dst[slot(i, v)] = acc
             prev, cur = cur, after_of
 
-    def rounds(first, times):
-        count = half + ITERS - first
+    def rounds(first_sweep, times):
+        count = half + ITERS - first_sweep
 
         @pl.loop(0, times)
         def _(_step):
@@ -682,10 +759,30 @@
         for k in range(LOW):
             pl.when(jnp.logical_not(home(n, k)))(word(n, k).wait_send)
 
+    pl.when(picks)(lambda: pick(0, quarter // 2))
     pl.when(picks)(lambda: post(0))
     if early:
-        pl.when(picks)(lambda: pick(1))
+        pl.when(picks)(lambda: pick(1, 0))
         pl.when(picks)(lambda: post(1))
+
+    for copy_of in time_copies:
+        copy_of.wait_send()
+    tally_send.wait_send()
+    for u in range(subs):
+        sends(me, u, True, True)
+        if early:
+            copy(3, me, u, corner, True).wait_send()
+        for k in range(1, reach + 1):
+            own_line(k, u, True)
+
+    @pl.loop(1, reach + 3)
+    def _(i):
+        side_turn(i, True, True)
+
+    @pl.when(owner)
+    def _():
+        seen_send.wait_send()
+        spot_send.wait_send()
 
     def word_in(n, side):
         return remote(
@@ -707,21 +804,6 @@
     if early:
         pl.when(picks)(lambda: posted(1))
     stay.wait()
-    for copy_of in time_copies:
-        copy_of.wait_send()
-    tally_send.wait_send()
-    sends(me, True, True)
-    for k in range(1, reach + 1):
-        own_line(k, True)
-
-    @pl.loop(1, reach + 3)
-    def _(i):
-        turn(i, True)
-
-    @pl.when(owner)
-    def _():
-        seen_send.wait_send()
-        spot_send.wait_send()
 
 
 def finish_kernel(cores, slots_ref, got_ref, own_ref, out_ref, arr_ref):
@@ -775,6 +857,7 @@
     ring_shape = ((ring + 2) * rows, 8, cells_z)
     span_shape = ((span + 2) * rows, 8, cells_z)
     dma = pltpu.SemaphoreType.DMA
+    subs = 1
     slots, got, own = pl.pallas_call(
         functools.partial(solve_kernel, bricks, cores),
         name="solve",
@@ -813,10 +896,10 @@
             pltpu.SMEM((2,), i32),
             pltpu.SMEM((2,), i32),
             pltpu.SMEM((2,), i32),
-            dma((2, bricks // LOW)),
-            dma((4, bricks)),
-            dma((bricks,)),
-            dma((bricks,)),
+            dma((2, bricks // LOW, subs)),
+            dma((4, bricks, subs)),
+            dma((bricks, subs)),
+            dma((bricks, subs)),
             dma,
             dma((7,)),
             dma((3,)),

time: 41.1 us -> 39.4 us (0.959)
  Pallas kernels: 39.9 us -> 38.6 us
    pallas_call x1, Pallas kernels: 39.1 us -> 37.8 us  [per_device(): pl.pallas_call(functools.partial(solve_kernel, bricks, cores), name='solv...]
where the time goes in v5:
time: 39.4 us; the launch traced here: 39.2 us
  Pallas kernels  38.6 us (98%)
  between operations  0.64 us (2%)
    pallas_call x1, Pallas kernels, per_device(): pl.pallas_call(functools.partial(solve_kernel, bricks, cores), name='solv...  37.8 us
    pallas_call x1, Pallas kernels, per_device(): pl.pallas_call(functools.partial(finish_kernel, cores), name='finish', ou...  0.79 us

profile of v5, /device:TPU:0, one launch (start us, length us, event | category | flops | bytes accessed | tf_op | source)
XLA Modules:
  0.0 39.2 jit_solution(5104141990558670533)
XLA Ops:
  0.6 37.8 %solve.1 = (f32[8,2,32,128]{3,2,1,0:T(8,128)S(1)}, f32[2,2,1,128]{3,2,1,0:T(1,128)S(1)}, f32[4,32,128]{2,1,0:T(8,128)S(1)}) custom-call(f32[4,64,128]{2,1,0:T(8,128)} %slow_ref.1, s32[2]{0:T(128)} %sx_ref.1, s32[2]{0:T(128)} %sy_ref.1, s32[2]{0:T(128)} %sz_ref.1, s32[1,2048]{1,0:T(1,128)} %bitcast.3, s32[1,2048]{1,0:T(1,128)} %bitcast.4, s32[1,2048]{1,0:T(1,128)} %bitcast.5, ...), custom_call_target="tpu_custom_call" | custom-call | tf_op jit(solution)/shard_map/solve/pallas_call | solution.py:861
  38.5 0.8 %finish.1 = (f32[4,32,128]{2,1,0:T(8,128)}, f32[2,128]{1,0:T(2,128)}) custom-call(f32[8,2,32,128]{3,2,1,0:T(8,128)S(1)} %get-tuple-element.5.slots_ref, f32[2,2,1,128]{3,2,1,0:T(1,128)S(1)} %get-tuple-element.6.got_ref, f32[4,32,128]{2,1,0:T(8,128)S(1)} %get-tuple-element.7.own_ref), custom_call_target="tpu_custom_call" | custom-call | tf_op jit(solution)/shard_map/finish/pallas_call | solution.py:936
